TPU v7x, 512 devices: a whole 4x8x8 slice. The times are simulated.
512 devices in a mesh: row: 16 (over y, core), col: 32 (over x, z).
Axes of the slice: x: 4, y: 8, z: 8, core: 2. Of those that a mesh axis runs over, the one named last changes fastest.
Arguments:
- vectors: bfloat16 [16, 32, 128, 384], P('row', 'col'), may hold values from -6 to 6
- near_blocks: bfloat16 [16, 32, 9, 384, 384], P('row', 'col'), may hold values from -0.15625 to 0.15625
- near_source: int32 [16, 32, 9], P('row', 'col'), may hold values from 0 to 8, each once within a row
- near_count: int32 [16, 32], P('row', 'col'), may hold values from 1 to 9
- basis_col: bfloat16 [16, 32, 64, 384], P('row', 'col'), may hold values from -0.3125 to 0.3125
- transfer_col: bfloat16 [16, 32, 64, 64], P('row', 'col'), may hold values from -0.125 to 0.125
- leaf_couple: bfloat16 [16, 32, 3, 29, 64, 64], P('row', 'col'), may hold values from -0.078125 to 0.078125
- coupling: bfloat16 [16, 16, 64, 64], P('row'), may hold values from -0.21875 to 0.21875
- distant_region_list: int32 [16, 16], P('row'), may hold values from 0 to 15, each once within a row
- transfer_row: bfloat16 [16, 32, 64, 64], P('row', 'col'), may hold values from -0.75 to 0.75
- basis_row: bfloat16 [16, 32, 64, 384], P('row', 'col'), may hold values from -0.75 to 0.75
Outputs:
- product: bfloat16 [16, 32, 128, 384], P('row', 'col')
Inputs may be any that keep to these rules, and one draw needn't show every extreme that they name: `near_source`: the 9 slots of a leaf name the nine neighbourhood cells once each. Only the first near_count slots of a leaf are live. `distant_region_list`: each region's list names every region once.
All inputs are finite; a program needn't handle non-finite values.
Results may differ from a plain program's by a relative error of at most 0.013.
Values may be sent and summed in bfloat16 or wider, within the bound.
No kernel may reach another device: no remote copies, remote signals or barrier semaphores. Data moves between devices by JAX's collectives and lax.ppermute only.
A program may use at most 64 MiB of HBM per device.

v0:
```python
import jax
import jax.numpy as jnp
from jax import lax
from jax.sharding import PartitionSpec as P


def from_behind(value, axis, steps):
    count = lax.axis_size(axis)
    pairs = [(source, (source + steps) % count) for source in range(count)]
    return lax.ppermute(value, axis, pairs)


def padded_2(cells, sides, width):
    for axis, dim in sides:
        count = lax.axis_size(axis)
        head = lax.slice_in_dim(cells, 0, width, axis=dim)
        tail = lax.slice_in_dim(cells, cells.shape[dim] - width, cells.shape[dim], axis=dim)
        cells = jnp.concatenate(
            [
                lax.ppermute(tail, axis, [(i, (i + 1) % count) for i in range(count)]),
                cells,
                lax.ppermute(head, axis, [((i + 1) % count, i) for i in range(count)]),
            ],
            axis=dim,
        )
    return cells


def from_everyone(shard, axis):
    copies = jnp.broadcast_to(shard, (lax.axis_size(axis), *shard.shape))
    return lax.all_to_all(copies, axis, split_axis=0, concat_axis=0, tiled=True)


def taken_together(shard, axis):
    return from_everyone(shard, axis).astype(jnp.float32).sum(axis=0)


def laid_out(blocks, dim):
    blocks = jnp.moveaxis(blocks, 0, dim)
    lengths = blocks.shape
    return blocks.reshape(*lengths[:dim], lengths[dim] * lengths[dim + 1], *lengths[dim + 2 :])


def collect(shard, axis, dim):
    return laid_out(from_everyone(shard, axis), dim)


def per_device(
    vectors,
    near_blocks,
    near_source,
    near_count,
    basis_col,
    transfer_col,
    leaf_couple,
    coupling,
    distant_region_list,
    transfer_row,
    basis_row,
):
    upper_limit = lax.Precision.HIGHEST
    leading = from_behind(vectors, "row", -1)
    leading = from_behind(leading, "col", -1)
    padded = padded_2(leading, (("row", 0), ("col", 1)), 1)
    table = padded.reshape(9, padded.shape[2], padded.shape[3])
    picked = jnp.take(table, near_source[0, 0], axis=0)
    slots = jnp.arange(picked.shape[0], dtype=jnp.int32)
    live_mask = (slots < near_count[0, 0])[:, None, None]
    picked = jnp.where(live_mask, picked, jnp.zeros_like(picked))
    near_part = jnp.einsum(
        "svp,spq->vq", picked, near_blocks[0, 0], preferred_element_type=jnp.float32
    )
    incoming_leaf = lax.dot_general(
        vectors[0, 0], basis_col[0, 0], (((1,), (1,)), ((), ())), preferred_element_type=jnp.float32
    )
    next_row = from_behind(incoming_leaf.astype(jnp.bfloat16), "row", -1).astype(
        incoming_leaf.dtype
    )
    second_row = from_behind(incoming_leaf.astype(jnp.bfloat16), "row", -2).astype(
        incoming_leaf.dtype
    )
    three_rows = jnp.stack([incoming_leaf, next_row, second_row], axis=0)
    leaves_of_rows = lax.all_gather(
        three_rows[:, None].astype(jnp.bfloat16), "col", axis=1, tiled=True
    ).astype(jnp.float32)
    col_count = lax.axis_size("col")
    rolled = jnp.roll(leaves_of_rows, -(lax.axis_index("col") + 3), axis=1)[:, : col_count - 3]
    band = jnp.einsum(
        "dfvk,dfkl->vl", rolled, leaf_couple[0, 0].astype(jnp.float32), precision=upper_limit
    )
    upward = jnp.dot(incoming_leaf, transfer_col[0, 0].astype(jnp.float32), precision=upper_limit)
    row_count = lax.axis_size("row")
    own_region = taken_together(upward.astype(jnp.bfloat16), "col").astype(jnp.float32)
    regions = collect(own_region[None].astype(jnp.bfloat16), "row", 0).astype(jnp.float32)
    listing = distant_region_list[0]
    far_mask = ((listing - lax.axis_index("row")) % row_count >= 3).astype(jnp.float32)
    far_coeff = jnp.take(regions, listing, axis=0) * far_mask[:, None, None]
    outgoing_region = jnp.einsum(
        "fvk,fkl->vl", far_coeff, coupling[0].astype(jnp.float32), precision=upper_limit
    )
    leaf_out = band + jnp.dot(
        outgoing_region, transfer_row[0, 0].astype(jnp.float32), precision=upper_limit
    )
    far_part = jnp.dot(leaf_out, basis_row[0, 0].astype(jnp.float32), precision=upper_limit)
    return (near_part + far_part).astype(jnp.bfloat16)[None, None]


def solution(mesh):
    placed = (
        P("row", "col", None, None),
        P("row", "col", None, None, None),
        P("row", "col", None),
        P("row", "col"),
        P("row", "col", None, None),
        P("row", "col", None, None),
        P("row", "col", None, None, None, None),
        P("row", None, None, None),
        P("row", None),
        P("row", "col", None, None),
        P("row", "col", None, None),
    )
    return jax.shard_map(
        per_device,
        mesh=mesh,
        in_specs=placed,
        out_specs=P("row", "col", None, None),
        check_vma=False,
    )
```

profile of v0, /device:TPU:8, one launch (start us, length us, event | category | flops | bytes accessed | tf_op | source)
XLA Modules:
  0.0 112.7 jit_solution(446802460981137565)
XLA Ops:
  6.5 1.2 %fusion.48 = (bf16[128,64]{0,1:T(8,128)(2,1)S(1)}, f32[128,64]{0,1:T(8,128)S(1)}) fusion(bf16[1,1,64,384]{3,2,1,0:T(8,128)(2,1)} %param.15, bf16[1,1,128,384]{3,2,1,0:T(8,128)(2,1)} %param.11), kind=kOutput, calls=%fused_computation.64 | convolution fusion | flops 6299648 | bytes 196608 | tf_op jit(solution)/shard_map/dot_general | solution.py:73
  7.8 7.7 %collective-permute-start.7 = (bf16[128,64]{0,1:T(8,128)(2,1)S(1)}, bf16[128,64]{0,1:T(8,128)(2,1)S(1)}, u32[]{:S(2)}, u32[]{:S(2)}) collective-permute-start(bf16[128,64]{0,1:T(8,128)(2,1)S(1)} %get-tuple-element.7), channel_id=1, source_target_pairs={{0,448},{32,480},{64,0},{96,32},{128,64},{160,96},{192,128},{224,1... | collective-permute-start | bytes 49160 | tf_op jit(solution)/shard_map/ppermute | solution.py:10
  15.5 1.4 %collective-permute-done.7 = bf16[128,64]{0,1:T(8,128)(2,1)S(1)} collective-permute-done((bf16[128,64]{0,1:T(8,128)(2,1)S(1)}, bf16[128,64]{0,1:T(8,128)(2,1)S(1)}, u32[]{:S(2)}, u32[]{:S(2)}) %collective-permute-start.7) | collective-permute-done | bytes 16416 | tf_op jit(solution)/shard_map/ppermute | solution.py:10
  17.7 1.9 %collective-permute-start = (bf16[1,1,128,384]{3,2,1,0:T(8,128)(2,1)}, bf16[1,1,128,384]{3,2,1,0:T(8,128)(2,1)S(1)}, u32[]{:S(2)}, u32[]{:S(2)}) collective-permute-start(bf16[1,1,128,384]{3,2,1,0:T(8,128)(2,1)} %param.11), channel_id=1, source_target_pairs={{0,480},{32,0},{64,32},{96,64},{128,96},{160,128},{192,160},{224,1... | collective-permute-start | bytes 294920 | tf_op jit(solution)/shard_map/ppermute | solution.py:10
  19.6 0.9 convolution_convert_fusion
  20.5 0.9 broadcast_in_dim.49
  21.4 10.2 %all-to-all-start = ((bf16[32,128,64]{1,2,0:T(8,128)(2,1)}), bf16[32,128,64]{1,2,0:T(8,128)(2,1)S(1)}, u32[]{:S(2)}, u32[]{:S(2)}) async-start(bf16[32,128,64]{1,2,0:T(8,128)(2,1)} %broadcast_in_dim.49), calls=%async_computation | async-start | bytes 1048576 | tf_op jit(solution)/shard_map/all_to_all | solution.py:31
  32.9 7.1 %collective-permute-start.1 = (bf16[1,1,128,384]{3,2,1,0:T(8,128)(2,1)S(1)}, bf16[1,1,128,384]{3,2,1,0:T(8,128)(2,1)S(1)}, u32[]{:S(2)}, u32[]{:S(2)}) collective-permute-start(bf16[1,1,128,384]{3,2,1,0:T(8,128)(2,1)S(1)} %collective-permute-done), channel_id=1, source_target_pairs={{0,31},{1,0},{2,1},{3,2},{4,3},{5,4},{6,5},{7,6},{8,7},{9,8},{10,9... | collective-permute-start | bytes 294920 | tf_op jit(solution)/shard_map/ppermute | solution.py:10
  40.0 6.6 %collective-permute-done.1 = bf16[1,1,128,384]{3,2,1,0:T(8,128)(2,1)S(1)} collective-permute-done((bf16[1,1,128,384]{3,2,1,0:T(8,128)(2,1)S(1)}, bf16[1,1,128,384]{3,2,1,0:T(8,128)(2,1)S(1)}, u32[]{:S(2)}, u32[]{:S(2)}) %collective-permute-start.1) | collective-permute-done | bytes 98336 | tf_op jit(solution)/shard_map/ppermute | solution.py:10
  46.7 1.7 %collective-permute-start.3 = (bf16[1,1,128,384]{3,2,1,0:T(8,128)(2,1)S(1)}, bf16[1,1,128,384]{3,2,1,0:T(8,128)(2,1)S(1)}, u32[]{:S(2)}, u32[]{:S(2)}) collective-permute-start(bf16[1,1,128,384]{3,2,1,0:T(8,128)(2,1)S(1)} %collective-permute-done.1), channel_id=1, source_target_pairs={{32,0},{64,32},{96,64},{128,96},{160,128},{192,160},{224,192},{256... | collective-permute-start | bytes 294920 | tf_op jit(solution)/shard_map/ppermute | solution.py:22
  48.4 2.3 %collective-permute-done.2 = bf16[1,1,128,384]{3,2,1,0:T(8,128)(2,1)S(1)} collective-permute-done((bf16[1,1,128,384]{3,2,1,0:T(8,128)(2,1)S(1)}, bf16[1,1,128,384]{3,2,1,0:T(8,128)(2,1)S(1)}, u32[]{:S(2)}, u32[]{:S(2)}) %collective-permute-start.2) | collective-permute-done | bytes 98336 | tf_op jit(solution)/shard_map/ppermute | solution.py:20
  50.8 5.5 %collective-permute-start.5 = (bf16[3,1,128,384]{3,2,1,0:T(8,128)(2,1)S(1)}, bf16[3,1,128,384]{3,2,1,0:T(8,128)(2,1)}, u32[]{:S(2)}, u32[]{:S(2)}) collective-permute-start(bf16[3,1,128,384]{3,2,1,0:T(8,128)(2,1)S(1)} %constant_dynamic-update-slice_fusion), channel_id=1, source_target_pairs={{1,0},{2,1},{3,2},{4,3},{5,4},{6,5},{7,6},{8,7},{9,8},{10,9},{11,1... | collective-permute-start | bytes 884744 | tf_op jit(solution)/shard_map/ppermute | solution.py:22
  56.3 1.9 %collective-permute-start.4 = (bf16[3,1,128,384]{3,2,1,0:T(8,128)(2,1)S(1)}, bf16[3,1,128,384]{3,2,1,0:T(8,128)(2,1)}, u32[]{:S(2)}, u32[]{:S(2)}) collective-permute-start(bf16[3,1,128,384]{3,2,1,0:T(8,128)(2,1)S(1)} %constant_dynamic-update-slice_fusion), channel_id=1, source_target_pairs={{0,1},{1,2},{2,3},{3,4},{4,5},{5,6},{6,7},{7,8},{8,9},{9,10},{10,1... | collective-permute-start | bytes 884744 | tf_op jit(solution)/shard_map/ppermute | solution.py:20
  58.3 0.8 broadcast_in_dim.50
  59.1 8.2 %all-to-all-start.1 = ((bf16[16,1,128,64]{2,3,1,0:T(8,128)(2,1)}), bf16[16,1,128,64]{2,3,1,0:T(8,128)(2,1)}, u32[]{:S(2)}, u32[]{:S(2)}) async-start(bf16[16,1,128,64]{2,3,1,0:T(8,128)(2,1)} %broadcast_in_dim.50), calls=%async_computation.1 | async-start | bytes 524288 | tf_op jit(solution)/shard_map/all_to_all | solution.py:31
  67.3 4.0 %collective-permute-done.4 = bf16[3,1,128,384]{3,2,1,0:T(8,128)(2,1)} collective-permute-done((bf16[3,1,128,384]{3,2,1,0:T(8,128)(2,1)S(1)}, bf16[3,1,128,384]{3,2,1,0:T(8,128)(2,1)}, u32[]{:S(2)}, u32[]{:S(2)}) %collective-permute-start.4) | collective-permute-done | bytes 294944 | tf_op jit(solution)/shard_map/ppermute | solution.py:20
  71.3 1.3 %pad_maximum_fusion = bf16[3,3,128,384]{3,2,1,0:T(8,128)(2,1)S(1)} fusion(bf16[3,1,128,384]{3,2,1,0:T(8,128)(2,1)} %collective-permute-done.5, bf16[3,1,128,384]{3,2,1,0:T(8,128)(2,1)} %copy-done.1, bf16[3,1,128,384]{3,2,1,0:T(8,128)(2,1)} %collective-permute-done.4), kind=kLoop, calls=%fused_computation.17 | loop fusion | flops 884736 | bytes 1769472 | tf_op jit(solution)/shard_map/concatenate | solution.py:18
  72.5 1.7 %gather_fusion = bf16[9,128,384]{2,1,0:T(8,128)(2,1)} fusion(bf16[9,128,384]{2,1,0:T(8,128)(2,1)S(1)} %bitcast.73, s32[1024]{0:T(1024)S(1)} %pad_clamp_fusion.1), kind=kCustom, calls=%fused_computation | custom fusion | bytes 1769508 | tf_op jit(solution)/shard_map/jit(_take)/gather | solution.py:66
  74.2 2.5 %fusion.6 = f32[128,384]{1,0:T(8,128)} fusion(bf16[1,1,9,384,384]{4,3,2,1,0:T(8,128)(2,1)S(1)} %copy-done, bf16[9,128,384]{2,1,0:T(8,128)(2,1)} %gather_fusion, pred[9]{0:T(512)(128)(4,1)} %get-tuple-element.9, pred[9]{0:T(512)(128)(4,1)} %get-tuple-element.10), kind=kOutput, calls=%fused_computation.10 | convolution fusion | flops 340623360 | bytes 3735570 | tf_op jit(solution)/shard_map/svp,spq->vq/dot_general | solution.py:70
  77.0 1.8 %bitcast_convert_fusion = f32[16,128,64]{1,2,0:T(8,128)} fusion(bf16[16,1,128,64]{2,3,1,0:T(8,128)(2,1)} %all-to-all-done.1), kind=kLoop, calls=%fused_computation.26 | loop fusion | flops 131072 | bytes 786432 | tf_op jit(solution)/shard_map/convert_element_type | solution.py:94
  78.8 1.6 %gather_fusion.1 = f32[16,128,64]{1,2,0:T(8,128)S(1)} fusion(f32[16,128,64]{1,2,0:T(8,128)} %bitcast_convert_fusion, s32[1024]{0:T(1024)S(1)} %pad_clamp_fusion), kind=kCustom, calls=%fused_computation.1 | custom fusion | bytes 1048640 | tf_op jit(solution)/shard_map/jit(_take)/gather | solution.py:97
  81.3 21.0 %all-gather.2.cloned.1.call-done = bf16[3,32,128,64]{2,3,1,0:T(8,128)(2,1)} async-done(((bf16[3,1,128,64]{2,3,1,0:T(8,128)(2,1)}), bf16[3,32,128,64]{2,3,1,0:T(8,128)(2,1)}) %all-gather.2.cloned.1.call-update) | async-done | bytes 1572880 | tf_op jit(solution)/shard_map/all_gather | solution.py:83
  102.4 2.6 %fusion.16 = f32[128,64]{1,0:T(8,128)S(1)} fusion(f32[128,64]{1,0:T(8,128)S(1)} %fusion.37, bf16[1,1,3,29,64,64]{5,4,3,2,1,0:T(8,128)(2,1)} %param.17, s32[]{:T(128)S(6)} %select_n.72, bf16[3,32,128,64]{2,3,1,0:T(8,128)(2,1)} %all-gather.2.cloned.1.call-done), kind=kOutput, calls=%fused_computation.15 | convolution fusion | flops 94380032 | bytes 2351108 | tf_op jit(solution)/shard_map/dfvk,dfkl->vl/dot_general | solution.py:88
  104.9 0.9 fusion.10
  (39 shorter events, 2.7 us)
Async XLA Ops:
  6.5 67.7 %copy-start = (bf16[1,1,9,384,384]{4,3,2,1,0:T(8,128)(2,1)S(1)}, bf16[1,1,9,384,384]{4,3,2,1,0:T(8,128)(2,1)}, u32[]{:S(2)}) copy-start(bf16[1,1,9,384,384]{4,3,2,1,0:T(8,128)(2,1)} %param.12) | copy-start | bytes 7962628
  6.5 25.7 %copy-start.6 = (s32[1,1,9]{2,1,0:T(1,128)S(1)}, s32[1,1,9]{2,1,0:T(1,128)}, u32[]{:S(2)}) copy-start(s32[1,1,9]{2,1,0:T(1,128)} %param.13) | copy-start | bytes 112
  6.5 26.3 %copy-start.7 = (s32[1,16]{1,0:T(1,128)S(1)}, s32[1,16]{1,0:T(1,128)}, u32[]{:S(2)}) copy-start(s32[1,16]{1,0:T(1,128)} %param.19) | copy-start | bytes 196
  6.5 95.8 %all-gather.2.cloned.1.call-start = ((), (), s32[]{:S(2)}) async-start(), calls=%async_computation.2 | async-start | bytes 1622016 | tf_op jit(solution)/shard_map/all_gather | solution.py:83
  7.8 9.2 %collective-permute-start.7 = (bf16[128,64]{0,1:T(8,128)(2,1)S(1)}, bf16[128,64]{0,1:T(8,128)(2,1)S(1)}, u32[]{:S(2)}, u32[]{:S(2)}) collective-permute-start(bf16[128,64]{0,1:T(8,128)(2,1)S(1)} %get-tuple-element.7), channel_id=1, source_target_pairs={{0,448},{32,480},{64,0},{96,32},{128,64},{160,96},{192,128},{224,1... | collective-permute-start | bytes 49160 | tf_op jit(solution)/shard_map/ppermute | solution.py:10
  15.5 1.6 %collective-permute-start.6 = (bf16[128,64]{0,1:T(8,128)(2,1)S(1)}, bf16[128,64]{0,1:T(8,128)(2,1)S(1)}, u32[]{:S(2)}, u32[]{:S(2)}) collective-permute-start(bf16[128,64]{0,1:T(8,128)(2,1)S(1)} %get-tuple-element.7), channel_id=1, source_target_pairs={{0,480},{32,0},{64,32},{96,64},{128,96},{160,128},{192,160},{224,1... | collective-permute-start | bytes 49160 | tf_op jit(solution)/shard_map/ppermute | solution.py:10
  17.7 15.2 %collective-permute-start = (bf16[1,1,128,384]{3,2,1,0:T(8,128)(2,1)}, bf16[1,1,128,384]{3,2,1,0:T(8,128)(2,1)S(1)}, u32[]{:S(2)}, u32[]{:S(2)}) collective-permute-start(bf16[1,1,128,384]{3,2,1,0:T(8,128)(2,1)} %param.11), channel_id=1, source_target_pairs={{0,480},{32,0},{64,32},{96,64},{128,96},{160,128},{192,160},{224,1... | collective-permute-start | bytes 294920 | tf_op jit(solution)/shard_map/ppermute | solution.py:10
  21.4 36.8 %all-to-all-start = ((bf16[32,128,64]{1,2,0:T(8,128)(2,1)}), bf16[32,128,64]{1,2,0:T(8,128)(2,1)S(1)}, u32[]{:S(2)}, u32[]{:S(2)}) async-start(bf16[32,128,64]{1,2,0:T(8,128)(2,1)} %broadcast_in_dim.49), calls=%async_computation | async-start | bytes 1048576 | tf_op jit(solution)/shard_map/all_to_all | solution.py:31
  32.9 13.8 %collective-permute-start.1 = (bf16[1,1,128,384]{3,2,1,0:T(8,128)(2,1)S(1)}, bf16[1,1,128,384]{3,2,1,0:T(8,128)(2,1)S(1)}, u32[]{:S(2)}, u32[]{:S(2)}) collective-permute-start(bf16[1,1,128,384]{3,2,1,0:T(8,128)(2,1)S(1)} %collective-permute-done), channel_id=1, source_target_pairs={{0,31},{1,0},{2,1},{3,2},{4,3},{5,4},{6,5},{7,6},{8,7},{9,8},{10,9... | collective-permute-start | bytes 294920 | tf_op jit(solution)/shard_map/ppermute | solution.py:10
  46.7 4.0 %collective-permute-start.2 = (bf16[1,1,128,384]{3,2,1,0:T(8,128)(2,1)S(1)}, bf16[1,1,128,384]{3,2,1,0:T(8,128)(2,1)S(1)}, u32[]{:S(2)}, u32[]{:S(2)}) collective-permute-start(bf16[1,1,128,384]{3,2,1,0:T(8,128)(2,1)S(1)} %collective-permute-done.1), channel_id=1, source_target_pairs={{0,32},{32,64},{64,96},{96,128},{128,160},{160,192},{192,224},{224... | collective-permute-start | bytes 294920 | tf_op jit(solution)/shard_map/ppermute | solution.py:20
  46.7 4.1 %collective-permute-start.3 = (bf16[1,1,128,384]{3,2,1,0:T(8,128)(2,1)S(1)}, bf16[1,1,128,384]{3,2,1,0:T(8,128)(2,1)S(1)}, u32[]{:S(2)}, u32[]{:S(2)}) collective-permute-start(bf16[1,1,128,384]{3,2,1,0:T(8,128)(2,1)S(1)} %collective-permute-done.1), channel_id=1, source_target_pairs={{32,0},{64,32},{96,64},{128,96},{160,128},{192,160},{224,192},{256... | collective-permute-start | bytes 294920 | tf_op jit(solution)/shard_map/ppermute | solution.py:22
  50.8 16.5 %copy-start.1 = (bf16[3,1,128,384]{3,2,1,0:T(8,128)(2,1)}, bf16[3,1,128,384]{3,2,1,0:T(8,128)(2,1)S(1)}, u32[]{:S(2)}) copy-start(bf16[3,1,128,384]{3,2,1,0:T(8,128)(2,1)S(1)} %constant_dynamic-update-slice_fusion) | copy-start | bytes 884740
  50.8 16.5 %collective-permute-start.5 = (bf16[3,1,128,384]{3,2,1,0:T(8,128)(2,1)S(1)}, bf16[3,1,128,384]{3,2,1,0:T(8,128)(2,1)}, u32[]{:S(2)}, u32[]{:S(2)}) collective-permute-start(bf16[3,1,128,384]{3,2,1,0:T(8,128)(2,1)S(1)} %constant_dynamic-update-slice_fusion), channel_id=1, source_target_pairs={{1,0},{2,1},{3,2},{4,3},{5,4},{6,5},{7,6},{8,7},{9,8},{10,9},{11,1... | collective-permute-start | bytes 884744 | tf_op jit(solution)/shard_map/ppermute | solution.py:22
  56.3 15.0 %collective-permute-start.4 = (bf16[3,1,128,384]{3,2,1,0:T(8,128)(2,1)S(1)}, bf16[3,1,128,384]{3,2,1,0:T(8,128)(2,1)}, u32[]{:S(2)}, u32[]{:S(2)}) collective-permute-start(bf16[3,1,128,384]{3,2,1,0:T(8,128)(2,1)S(1)} %constant_dynamic-update-slice_fusion), channel_id=1, source_target_pairs={{0,1},{1,2},{2,3},{3,4},{4,5},{5,6},{6,7},{7,8},{8,9},{9,10},{10,1... | collective-permute-start | bytes 884744 | tf_op jit(solution)/shard_map/ppermute | solution.py:20
  59.1 17.9 %all-to-all-start.1 = ((bf16[16,1,128,64]{2,3,1,0:T(8,128)(2,1)}), bf16[16,1,128,64]{2,3,1,0:T(8,128)(2,1)}, u32[]{:S(2)}, u32[]{:S(2)}) async-start(bf16[16,1,128,64]{2,3,1,0:T(8,128)(2,1)} %broadcast_in_dim.50), calls=%async_computation.1 | async-start | bytes 524288 | tf_op jit(solution)/shard_map/all_to_all | solution.py:31
  76.8 3.7 %copy-start.2 = (bf16[1,16,64,64]{3,2,1,0:T(8,128)(2,1)S(1)}, bf16[1,16,64,64]{3,2,1,0:T(8,128)(2,1)}, u32[]{:S(2)}) copy-start(bf16[1,16,64,64]{3,2,1,0:T(8,128)(2,1)} %param.18) | copy-start | bytes 393220
  78.8 2.3 %copy-start.5 = (bf16[1,1,64,64]{3,2,1,0:T(8,128)(2,1)S(1)}, bf16[1,1,64,64]{3,2,1,0:T(8,128)(2,1)}, u32[]{:S(2)}) copy-start(bf16[1,1,64,64]{3,2,1,0:T(8,128)(2,1)} %param.20) | copy-start | bytes 24580
  81.3 23.6 %copy-start.3 = (f32[128,384]{1,0:T(8,128)S(1)}, f32[128,384]{1,0:T(8,128)}, u32[]{:S(2)}) copy-start(f32[128,384]{1,0:T(8,128)} %fusion.6) | copy-start | bytes 589828
  81.3 23.6 %copy-start.4 = (bf16[1,1,64,384]{3,2,1,0:T(8,128)(2,1)S(1)}, bf16[1,1,64,384]{3,2,1,0:T(8,128)(2,1)}, u32[]{:S(2)}) copy-start(bf16[1,1,64,384]{3,2,1,0:T(8,128)(2,1)} %param.21) | copy-start | bytes 147460
Sparse Core Ops, SparseCore 0:
  17.8 84.4 all-gather.1
where the time goes:
time: 113 us
  starting transfers between devices  44.2 us (39%)
  waiting for transfers between devices  35.8 us (32%)
  between operations  14.3 us (13%)
  matrix products  8.93 us (8%)
  local copies, waits for them, and re-layouts  5.08 us (4%)
  other arithmetic  4.39 us (4%)
    all_gather x1, waiting for transfers between devices, per_device(): lax.all_gather(three_rows[:, None].astype(jnp.bfloat16), 'col', axis=1, t...  21 us
    all_to_all x2, starting transfers between devices, from_everyone(): return lax.all_to_all(copies, axis, split_axis=0, concat_axis=0, tiled=True)  18.3 us
    ppermute x4, starting transfers between devices, from_behind(): return lax.ppermute(value, axis, pairs)  16.7 us
    ppermute x4, waiting for transfers between devices, from_behind(): return lax.ppermute(value, axis, pairs)  8.19 us
    ppermute x2, starting transfers between devices, padded_2(): lax.ppermute(head, axis, [((i + 1) % count, i) for i in range(count)])  7.21 us
    ppermute x2, waiting for transfers between devices, padded_2(): lax.ppermute(tail, axis, [(i, (i + 1) % count) for i in range(count)])  6.28 us
    dot_general x1, matrix products, per_device(): jnp.einsum('dfvk,dfkl->vl', rolled, leaf_couple[0, 0].astype(jnp.float32)...  2.56 us
    dot_general x1, matrix products, per_device(): jnp.einsum('svp,spq->vq', picked, near_blocks[0, 0], preferred_element_ty...  2.55 us
  transfers between devices with their start and end apart: 11, of which 7 were waited for; matrix products, arithmetic and copies ran while one was open for 12% of the time, Pallas kernels for 0%

commit v1 on v0

v1 whole, which is shorter than its diff:
```python
import jax
import jax.numpy as jnp
from jax import lax
from jax.experimental import pallas as pl
from jax.experimental.pallas import tpu as pltpu
from jax.sharding import PartitionSpec as P

VMEM = pltpu.VMEM
SMEM = pltpu.SMEM
HALF_BAND = 15


def shifted(value, axis, steps):
    count = lax.axis_size(axis)
    return lax.ppermute(value, axis, [((i + steps) % count, i) for i in range(count)])


def contract_rows(left, right):
    return lax.dot_general(left, right, (((0,), (0,)), ((), ())), preferred_element_type=jnp.float32)


def exact_rows(left, right):
    high = right.astype(jnp.bfloat16)
    low = (right - high.astype(jnp.float32)).astype(jnp.bfloat16)
    return contract_rows(left, high) + contract_rows(left, low)


def leaf_kernel(vectors, basis, transfer, out):
    coeff = lax.dot_general(
        basis[0, 0], vectors[0, 0], (((1,), (1,)), ((), ())), preferred_element_type=jnp.float32
    ).astype(jnp.bfloat16)
    half = transfer.shape[2] // 2
    packed = jnp.concatenate([transfer[0, 0, :half], transfer[0, 0, half:]], axis=1)
    chunk = jnp.concatenate([coeff, packed], axis=0)
    for i in range(out.shape[0]):
        out[i] = chunk


def pack_kernel(first, second, out_first, out_second):
    for source, out in ((first, out_first), (second, out_second)):
        bands, rank = source.shape[3], source.shape[4]
        left = source[0, 0, 0, :HALF_BAND].reshape(HALF_BAND * rank, rank)
        right = source[0, 0, 0, HALF_BAND:].reshape((bands - HALF_BAND) * rank, rank)
        right = jnp.concatenate([right, jnp.zeros(((2 * HALF_BAND - bands) * rank, rank), right.dtype)], axis=0)
        out[...] = jnp.concatenate([left, right], axis=1)


def mid_kernel(place, gathered, own, first, second, out, turned):
    row, col = place[0], place[1]
    cols, rank = gathered.shape[0], own.shape[4]
    rows = out.shape[0]
    bands = own.shape[3]
    for j in range(cols):
        turned[j * rank : (j + 1) * rank] = gathered[lax.rem(col + 3 + j, cols), :rank]
    half = rank // 2
    low = gathered[:, :half].reshape(cols * half, -1)
    high = gathered[:, half:rank].reshape(cols * half, -1)
    packed = gathered[:, rank:].reshape(cols * half, -1)
    region = contract_rows(packed[:, :rank], low) + contract_rows(packed[:, rank:], high)
    region = region.astype(out.dtype)
    for a in range(rows):
        out[a] = region
    out[row] = contract_rows(own[0, 0, 0].reshape(bands * rank, rank), turned[: bands * rank]).astype(out.dtype)
    size = HALF_BAND * rank
    for d, weights in ((1, first), (2, second)):
        term = contract_rows(weights[:, :rank], turned[:size]) + contract_rows(
            weights[:, rank:], turned[size : 2 * size]
        )
        out[lax.rem(row + rows - d, rows)] = term.astype(out.dtype)


def near_kernel(source, count, blocks, here, one, two, out, slot_of):
    slots = blocks.shape[2]
    for s in range(slots):
        slot_of[source[0, 0, s]] = s
    live_count = count[0, 0]
    out[...] = jnp.zeros_like(out)
    for cell in range(slots):
        bundle = (here, one, two)[cell // 3]
        slot = slot_of[cell]

        @pl.when(slot < live_count)
        def _():
            out[...] += jnp.dot(bundle[cell % 3], blocks[0, 0, slot], preferred_element_type=jnp.float32)


def final_kernel(place, listing, received, coupling, transfer, basis, near, out, terms):
    row = place[0]
    rows, rank = received.shape[0], received.shape[1]
    band = jnp.zeros(received.shape[1:], jnp.float32)
    for f in range(rows):
        region = listing[0, f]
        part = received[region]
        is_far = lax.rem(region - row + rows, rows) >= 3
        terms[f * rank : (f + 1) * rank] = jnp.where(is_far, part, jnp.zeros_like(part))
        band += jnp.where(is_far, jnp.zeros_like(part), part).astype(jnp.float32)
    outgoing = contract_rows(coupling[0].reshape(rows * rank, rank), terms[...])
    leaf_out = band + exact_rows(transfer[0, 0], outgoing)
    high = leaf_out.astype(jnp.bfloat16)
    low = (leaf_out - high.astype(jnp.float32)).astype(jnp.bfloat16)
    far = contract_rows(high, basis[0, 0]) + contract_rows(low, basis[0, 0])
    out[0, 0] = (near[...] + far).astype(out.dtype)


def call(kernel, out_shape, in_specs, scratch, cost, name):
    return pl.pallas_call(
        kernel,
        out_shape=out_shape,
        in_specs=in_specs,
        out_specs=jax.tree.map(lambda _: pl.BlockSpec(memory_space=VMEM), out_shape),
        scratch_shapes=scratch,
        cost_estimate=pl.CostEstimate(flops=cost[0], bytes_accessed=cost[1], transcendentals=0),
        compiler_params=pltpu.CompilerParams(vmem_limit_bytes=24 * 1024 * 1024),
        name=name,
    )


def per_device(
    vectors,
    near_blocks,
    near_source,
    near_count,
    basis_col,
    transfer_col,
    leaf_couple,
    coupling,
    distant_region_list,
    transfer_row,
    basis_row,
):
    rows, cols = lax.axis_size("row"), lax.axis_size("col")
    vecs, leaf = vectors.shape[2:]
    rank = basis_col.shape[2]
    bands = leaf_couple.shape[3]
    bf16, f32 = jnp.bfloat16, jnp.float32
    vmem, smem = pl.BlockSpec(memory_space=VMEM), pl.BlockSpec(memory_space=SMEM)
    place = jnp.stack([lax.axis_index("row"), lax.axis_index("col")]).astype(jnp.int32)

    col_one = shifted(vectors[0, 0], "col", 1)
    col_two = shifted(vectors[0, 0], "col", 2)

    chunks = call(
        leaf_kernel,
        jax.ShapeDtypeStruct((cols, rank + rank // 2, vecs), bf16),
        [vmem] * 3,
        [],
        (2 * rank * vecs * leaf, 2 * cols * 96 * vecs),
        "leaf",
    )(vectors, basis_col, transfer_col)
    gathered = lax.all_to_all(chunks, "col", split_axis=0, concat_axis=0, tiled=True)

    def slab(d):
        return pl.BlockSpec((1, 1, 1, bands, rank, rank), lambda i: (0, 0, d, 0, 0, 0))

    packed_shape = jax.ShapeDtypeStruct((HALF_BAND * rank, 2 * rank), bf16)
    first, second = pl.pallas_call(
        pack_kernel,
        grid=(1,),
        out_shape=[packed_shape] * 2,
        in_specs=[slab(1), slab(2)],
        out_specs=[pl.BlockSpec(packed_shape.shape, lambda i: (0, 0))] * 2,
        cost_estimate=pl.CostEstimate(flops=0, bytes_accessed=2000000, transcendentals=0),
        name="pack",
    )(leaf_couple, leaf_couple)
    first = shifted(first, "row", -1)
    second = shifted(second, "row", -2)

    here = jnp.stack([vectors[0, 0], col_one, col_two])
    row_one = shifted(here, "row", 1)
    row_two = shifted(here, "row", 2)

    outgoing = pl.pallas_call(
        mid_kernel,
        grid=(1,),
        out_shape=jax.ShapeDtypeStruct((rows, rank, vecs), bf16),
        in_specs=[
            smem,
            pl.BlockSpec((cols, rank + rank // 2, vecs), lambda i: (0, 0, 0)),
            slab(0),
            pl.BlockSpec(packed_shape.shape, lambda i: (0, 0)),
            pl.BlockSpec(packed_shape.shape, lambda i: (0, 0)),
        ],
        out_specs=pl.BlockSpec((rows, rank, vecs), lambda i: (0, 0, 0)),
        scratch_shapes=[VMEM((cols * rank, vecs), bf16)],
        cost_estimate=pl.CostEstimate(flops=2 * 2048 * 256 * 128, bytes_accessed=3000000, transcendentals=0),
        compiler_params=pltpu.CompilerParams(vmem_limit_bytes=24 * 1024 * 1024),
        name="mid",
    )(place, gathered, leaf_couple, first, second)
    received = lax.all_to_all(outgoing, "row", split_axis=0, concat_axis=0, tiled=True)

    near = call(
        near_kernel,
        jax.ShapeDtypeStruct((vecs, leaf), f32),
        [smem, smem, vmem, vmem, vmem, vmem],
        [SMEM((near_blocks.shape[2],), jnp.int32)],
        (2 * 9 * vecs * leaf * leaf, 2 * 9 * leaf * (leaf + vecs)),
        "near",
    )(near_source, near_count, near_blocks, here, row_one, row_two)

    return call(
        final_kernel,
        jax.ShapeDtypeStruct((1, 1, vecs, leaf), bf16),
        [smem, smem, vmem, vmem, vmem, vmem, vmem],
        [VMEM((rows * rank, vecs), bf16)],
        (2 * 1024 * 64 * 128 + 4 * 64 * 128 * 384, 1000000),
        "final",
    )(place, distant_region_list, received, coupling, transfer_row, basis_row, near)


def solution(mesh):
    placed = (
        P("row", "col", None, None),
        P("row", "col", None, None, None),
        P("row", "col", None),
        P("row", "col"),
        P("row", "col", None, None),
        P("row", "col", None, None),
        P("row", "col", None, None, None, None),
        P("row", None, None, None),
        P("row", None),
        P("row", "col", None, None),
        P("row", "col", None, None),
    )
    return jax.shard_map(
        per_device,
        mesh=mesh,
        in_specs=placed,
        out_specs=P("row", "col", None, None),
        check_vma=False,
    )
```

time: 113 us -> 74.7 us (0.66)
  the two profiles are of different devices: /device:TPU:8 before, /device:TPU:24 now
where the time goes in v1:
time: 74.7 us; the launch traced here: 74.1 us
  starting transfers between devices  39.6 us (53%)
  waiting for transfers between devices  20.4 us (27%)
  Pallas kernels  8.87 us (12%)
  local copies, waits for them, and re-layouts  4.29 us (6%)
  between operations  0.78 us (1%)
    ppermute x6, starting transfers between devices, shifted(): lax.ppermute(value, axis, [((i + steps) % count, i) for i in range(count)])  19 us
    ppermute x6, waiting for transfers between devices, shifted(): lax.ppermute(value, axis, [((i + steps) % count, i) for i in range(count)])  15.5 us
    all_to_all x1, starting transfers between devices, per_device(): lax.all_to_all(chunks, 'col', split_axis=0, concat_axis=0, tiled=True)  13.2 us
    all_to_all x1, starting transfers between devices, per_device(): lax.all_to_all(outgoing, 'row', split_axis=0, concat_axis=0, tiled=True)  7.48 us
    all_to_all x1, waiting for transfers between devices, per_device(): lax.all_to_all(chunks, 'col', split_axis=0, concat_axis=0, tiled=True)  4.95 us
    unnamed x22, local copies, waits for them, and re-layouts  4.29 us
    pallas_call x1, Pallas kernels, per_device(): pl.pallas_call(mid_kernel, grid=(1,), out_shape=jax.ShapeDtypeStruct((row...  2.21 us
    pallas_call x1, Pallas kernels, per_device(): pl.pallas_call(pack_kernel, grid=(1,), out_shape=[packed_shape] * 2, in_s...  2.1 us
  transfers between devices with their start and end apart: 8, of which 3 were waited for; matrix products, arithmetic and copies ran while one was open for 0% of the time, Pallas kernels for 8%

profile of v1, /device:TPU:24, one launch (start us, length us, event | category | flops | bytes accessed | tf_op | source)
XLA Modules:
  0.0 74.1 jit_solution(13770343606450067597)
XLA Ops:
  0.0 1.0 %copy-done.2 = bf16[1,1,128,384]{3,2,1,0:T(8,128)(2,1)S(1)} copy-done((bf16[1,1,128,384]{3,2,1,0:T(8,128)(2,1)S(1)}, bf16[1,1,128,384]{3,2,1,0:T(8,128)(2,1)}, u32[]{:S(2)}) %copy-start.2) | copy-done | bytes 98328
  1.0 0.8 %copy-done.5 = bf16[1,1,64,384]{3,2,1,0:T(8,128)(2,1)S(1)} copy-done((bf16[1,1,64,384]{3,2,1,0:T(8,128)(2,1)S(1)}, bf16[1,1,64,384]{3,2,1,0:T(8,128)(2,1)}, u32[]{:S(2)}) %copy-start.5) | copy-done | bytes 49176
  1.8 0.7 copy-done.8
  2.5 1.1 %leaf.1 = bf16[32,96,128]{2,1,0:T(8,128)(2,1)} custom-call(bf16[1,1,128,384]{3,2,1,0:T(8,128)(2,1)S(1)} %copy-done.2, bf16[1,1,64,384]{3,2,1,0:T(8,128)(2,1)S(1)} %copy-done.5, bf16[1,1,64,64]{3,2,1,0:T(8,128)(2,1)S(1)} %copy-done.8), custom_call_target="tpu_custom_call" | custom-call | flops 6291456 | bytes 786432 | tf_op jit(solution)/shard_map/leaf/pallas_call | solution.py:142
  3.6 13.2 %all-to-all-start = ((bf16[32,96,128]{2,1,0:T(8,128)(2,1)}), bf16[32,96,128]{2,1,0:T(8,128)(2,1)S(1)}, u32[]{:S(2)}, u32[]{:S(2)}) async-start(bf16[32,96,128]{2,1,0:T(8,128)(2,1)} %leaf.1), calls=%async_computation | async-start | bytes 1572864 | tf_op jit(solution)/shard_map/all_to_all | solution.py:150
  16.8 2.1 %pack.1 = (bf16[960,128]{1,0:T(8,128)(2,1)}, bf16[960,128]{1,0:T(8,128)(2,1)}) custom-call(bf16[1,1,3,29,64,64]{5,4,3,2,1,0:T(8,128)(2,1)} %own.1, bf16[1,1,3,29,64,64]{5,4,3,2,1,0:T(8,128)(2,1)} %own.1), custom_call_target="tpu_custom_call" | custom-call | bytes 2000000 | tf_op jit(solution)/shard_map/pack/pallas_call | solution.py:156
  18.9 0.0 collective-permute-start
  18.9 4.8 %collective-permute-start.1 = (bf16[960,128]{1,0:T(8,128)(2,1)}, bf16[960,128]{1,0:T(8,128)(2,1)S(1)}, u32[]{:S(2)}, u32[]{:S(2)}) collective-permute-start(bf16[960,128]{1,0:T(8,128)(2,1)} %get-tuple-element.8), channel_id=1, source_target_pairs={{448,0},{480,32},{0,64},{32,96},{64,128},{96,160},{128,192},{160,2... | collective-permute-start | bytes 737288 | tf_op jit(solution)/shard_map/ppermute | solution.py:15
  23.7 8.0 %collective-permute-start.3 = (bf16[128,384]{1,0:T(8,128)(2,1)S(1)}, bf16[128,384]{1,0:T(8,128)(2,1)S(1)}, u32[]{:S(2)}, u32[]{:S(2)}) collective-permute-start(bf16[128,384]{1,0:T(8,128)(2,1)S(1)} %bitcast.6), channel_id=1, source_target_pairs={{2,0},{3,1},{4,2},{5,3},{6,4},{7,5},{8,6},{9,7},{10,8},{11,9},{12,... | collective-permute-start | bytes 294920 | tf_op jit(solution)/shard_map/ppermute | solution.py:15
  31.7 3.4 %collective-permute-start.2 = (bf16[128,384]{1,0:T(8,128)(2,1)S(1)}, bf16[128,384]{1,0:T(8,128)(2,1)S(1)}, u32[]{:S(2)}, u32[]{:S(2)}) collective-permute-start(bf16[128,384]{1,0:T(8,128)(2,1)S(1)} %bitcast.7), channel_id=1, source_target_pairs={{1,0},{2,1},{3,2},{4,3},{5,4},{6,5},{7,6},{8,7},{9,8},{10,9},{11,1... | collective-permute-start | bytes 294920 | tf_op jit(solution)/shard_map/ppermute | solution.py:15
  35.1 0.1 pad_add_fusion.place
  35.2 0.0 collective-permute-done.first
  35.2 0.0 collective-permute-done.1.second
  35.2 4.9 %all-to-all-done.gathered = bf16[32,96,128]{2,1,0:T(8,128)(2,1)S(1)} async-done(((bf16[32,96,128]{2,1,0:T(8,128)(2,1)}), bf16[32,96,128]{2,1,0:T(8,128)(2,1)S(1)}, u32[]{:S(2)}, u32[]{:S(2)}) %all-to-all-start) | async-done | bytes 786464 | tf_op jit(solution)/shard_map/all_to_all | solution.py:150
  40.1 2.2 %mid.1 = bf16[16,64,128]{2,1,0:T(8,128)(2,1)} custom-call(s32[2]{0:T(128)S(1)} %pad_add_fusion.place, bf16[32,96,128]{2,1,0:T(8,128)(2,1)S(1)} %all-to-all-done.gathered, bf16[1,1,3,29,64,64]{5,4,3,2,1,0:T(8,128)(2,1)S(1)} %copy-done, bf16[960,128]{1,0:T(8,128)(2,1)S(1)} %collective-permute-done.first, bf16[960,128]{1,0:T(8,128)(2,1)S(1)} %collective-permute-done.1.second), custom_call_target="tpu_custom_call" | custom-call | flops 134217728 | bytes 3000000 | tf_op jit(solution)/shard_map/mid/pallas_call | solution.py:172
  42.4 7.5 %all-to-all-start.1 = ((bf16[16,64,128]{2,1,0:T(8,128)(2,1)}), bf16[16,64,128]{2,1,0:T(8,128)(2,1)S(1)}, u32[]{:S(2)}, u32[]{:S(2)}) async-start(bf16[16,64,128]{2,1,0:T(8,128)(2,1)} %mid.1), calls=%async_computation.1 | async-start | bytes 524288 | tf_op jit(solution)/shard_map/all_to_all | solution.py:189
  49.8 0.0 collective-permute-done.3
  49.9 0.3 collective-permute-start.4
  50.2 2.5 %collective-permute-start.5 = (bf16[3,128,384]{2,1,0:T(8,128)(2,1)S(1)}, bf16[3,128,384]{2,1,0:T(8,128)(2,1)S(1)}, u32[]{:S(2)}, u32[]{:S(2)}) collective-permute-start(bf16[3,128,384]{2,1,0:T(8,128)(2,1)S(1)} %pad_maximum_fusion.here), channel_id=1, source_target_pairs={{64,0},{96,32},{128,64},{160,96},{192,128},{224,160},{256,192},{28... | collective-permute-start | bytes 884744 | tf_op jit(solution)/shard_map/ppermute | solution.py:15
  53.4 9.2 %collective-permute-done.4.one = bf16[3,128,384]{2,1,0:T(8,128)(2,1)S(1)} collective-permute-done((bf16[3,128,384]{2,1,0:T(8,128)(2,1)S(1)}, bf16[3,128,384]{2,1,0:T(8,128)(2,1)S(1)}, u32[]{:S(2)}, u32[]{:S(2)}) %collective-permute-start.4) | collective-permute-done | bytes 294944 | tf_op jit(solution)/shard_map/ppermute | solution.py:15
  62.5 6.3 %collective-permute-done.5.two = bf16[3,128,384]{2,1,0:T(8,128)(2,1)S(1)} collective-permute-done((bf16[3,128,384]{2,1,0:T(8,128)(2,1)S(1)}, bf16[3,128,384]{2,1,0:T(8,128)(2,1)S(1)}, u32[]{:S(2)}, u32[]{:S(2)}) %collective-permute-start.5) | collective-permute-done | bytes 294944 | tf_op jit(solution)/shard_map/ppermute | solution.py:15
  68.8 1.7 %copy-done.1 = bf16[1,1,9,384,384]{4,3,2,1,0:T(8,128)(2,1)S(1)} copy-done((bf16[1,1,9,384,384]{4,3,2,1,0:T(8,128)(2,1)S(1)}, bf16[1,1,9,384,384]{4,3,2,1,0:T(8,128)(2,1)}, u32[]{:S(2)}) %copy-start.1) | copy-done | bytes 2654232
  70.6 1.6 %near.1 = f32[128,384]{1,0:T(8,128)S(1)} custom-call(s32[1,1,9]{2,1,0:T(1,128)S(1)} %copy-done.9, s32[1,1]{1,0:T(1,128)S(6)} %copy.12.count, bf16[1,1,9,384,384]{4,3,2,1,0:T(8,128)(2,1)S(1)} %copy-done.1, bf16[3,128,384]{2,1,0:T(8,128)(2,1)S(1)} %pad_maximum_fusion.here, bf16[3,128,384]{2,1,0:T(8,128)(2,1)S(1)} %collective-permute-done.4.one, ...), custom_call_target="tpu_custom_call" | custom-call | flops 339738624 | bytes 3538944 | tf_op jit(solution)/shard_map/near/pallas_call | solution.py:191
  72.3 1.8 %final.1 = bf16[1,1,128,384]{3,2,1,0:T(8,128)(2,1)} custom-call(s32[2]{0:T(128)S(1)} %pad_add_fusion.place, s32[1,16]{1,0:T(1,128)S(1)} %copy-done.10, bf16[16,64,128]{2,1,0:T(8,128)(2,1)S(1)} %all-to-all-done.1.received, bf16[1,16,64,64]{3,2,1,0:T(8,128)(2,1)S(1)} %copy-done.4, bf16[1,1,64,64]{3,2,1,0:T(8,128)(2,1)S(1)} %copy-done.7, ...), custom_call_target="tpu_custom_call" | custom-call | flops 29360128 | bytes 1000000 | tf_op jit(solution)/shard_map/final/pallas_call | solution.py:200
  (21 shorter events, 0.1 us)
Async XLA Ops:
  0.0 40.1 %copy-start = (bf16[1,1,3,29,64,64]{5,4,3,2,1,0:T(8,128)(2,1)S(1)}, bf16[1,1,3,29,64,64]{5,4,3,2,1,0:T(8,128)(2,1)}, u32[]{:S(2)}) copy-start(bf16[1,1,3,29,64,64]{5,4,3,2,1,0:T(8,128)(2,1)} %own.1) | copy-start | bytes 2138116
  0.0 1.0 %copy-start.2 = (bf16[1,1,128,384]{3,2,1,0:T(8,128)(2,1)S(1)}, bf16[1,1,128,384]{3,2,1,0:T(8,128)(2,1)}, u32[]{:S(2)}) copy-start(bf16[1,1,128,384]{3,2,1,0:T(8,128)(2,1)} %vectors.1) | copy-start | bytes 294916
  1.0 0.8 %copy-start.5 = (bf16[1,1,64,384]{3,2,1,0:T(8,128)(2,1)S(1)}, bf16[1,1,64,384]{3,2,1,0:T(8,128)(2,1)}, u32[]{:S(2)}) copy-start(bf16[1,1,64,384]{3,2,1,0:T(8,128)(2,1)} %basis.2) | copy-start | bytes 147460
  1.8 0.7 copy-start.8
  2.5 21.2 %copy-start.3 = (bf16[1,1,128,384]{3,2,1,0:T(8,128)(2,1)S(1)}, bf16[1,1,128,384]{3,2,1,0:T(8,128)(2,1)}, u32[]{:S(2)}) copy-start(bf16[1,1,128,384]{3,2,1,0:T(8,128)(2,1)} %vectors.1) | copy-start | bytes 294916
  3.6 36.5 %all-to-all-start = ((bf16[32,96,128]{2,1,0:T(8,128)(2,1)}), bf16[32,96,128]{2,1,0:T(8,128)(2,1)S(1)}, u32[]{:S(2)}, u32[]{:S(2)}) async-start(bf16[32,96,128]{2,1,0:T(8,128)(2,1)} %leaf.1), calls=%async_computation | async-start | bytes 1572864 | tf_op jit(solution)/shard_map/all_to_all | solution.py:150
  18.9 50.0 %copy-start.9 = (s32[1,1,9]{2,1,0:T(1,128)S(1)}, s32[1,1,9]{2,1,0:T(1,128)}, u32[]{:S(2)}) copy-start(s32[1,1,9]{2,1,0:T(1,128)} %source.1) | copy-start | bytes 112
  18.9 16.3 %collective-permute-start = (bf16[960,128]{1,0:T(8,128)(2,1)}, bf16[960,128]{1,0:T(8,128)(2,1)S(1)}, u32[]{:S(2)}, u32[]{:S(2)}) collective-permute-start(bf16[960,128]{1,0:T(8,128)(2,1)} %get-tuple-element.7), channel_id=1, source_target_pairs={{480,0},{0,32},{32,64},{64,96},{96,128},{128,160},{160,192},{192,2... | collective-permute-start | bytes 737288 | tf_op jit(solution)/shard_map/ppermute | solution.py:15
  18.9 16.3 %collective-permute-start.1 = (bf16[960,128]{1,0:T(8,128)(2,1)}, bf16[960,128]{1,0:T(8,128)(2,1)S(1)}, u32[]{:S(2)}, u32[]{:S(2)}) collective-permute-start(bf16[960,128]{1,0:T(8,128)(2,1)} %get-tuple-element.8), channel_id=1, source_target_pairs={{448,0},{480,32},{0,64},{32,96},{64,128},{96,160},{128,192},{160,2... | collective-permute-start | bytes 737288 | tf_op jit(solution)/shard_map/ppermute | solution.py:15
  23.7 26.1 %collective-permute-start.3 = (bf16[128,384]{1,0:T(8,128)(2,1)S(1)}, bf16[128,384]{1,0:T(8,128)(2,1)S(1)}, u32[]{:S(2)}, u32[]{:S(2)}) collective-permute-start(bf16[128,384]{1,0:T(8,128)(2,1)S(1)} %bitcast.6), channel_id=1, source_target_pairs={{2,0},{3,1},{4,2},{5,3},{6,4},{7,5},{8,6},{9,7},{10,8},{11,9},{12,... | collective-permute-start | bytes 294920 | tf_op jit(solution)/shard_map/ppermute | solution.py:15
  31.7 18.1 %collective-permute-start.2 = (bf16[128,384]{1,0:T(8,128)(2,1)S(1)}, bf16[128,384]{1,0:T(8,128)(2,1)S(1)}, u32[]{:S(2)}, u32[]{:S(2)}) collective-permute-start(bf16[128,384]{1,0:T(8,128)(2,1)S(1)} %bitcast.7), channel_id=1, source_target_pairs={{1,0},{2,1},{3,2},{4,3},{5,4},{6,5},{7,6},{8,7},{9,8},{10,9},{11,1... | collective-permute-start | bytes 294920 | tf_op jit(solution)/shard_map/ppermute | solution.py:15
  42.3 29.9 %copy-start.4 = (bf16[1,16,64,64]{3,2,1,0:T(8,128)(2,1)S(1)}, bf16[1,16,64,64]{3,2,1,0:T(8,128)(2,1)}, u32[]{:S(2)}) copy-start(bf16[1,16,64,64]{3,2,1,0:T(8,128)(2,1)} %coupling.1) | copy-start | bytes 393220
  42.4 29.9 %copy-start.6 = (bf16[1,1,64,384]{3,2,1,0:T(8,128)(2,1)S(1)}, bf16[1,1,64,384]{3,2,1,0:T(8,128)(2,1)}, u32[]{:S(2)}) copy-start(bf16[1,1,64,384]{3,2,1,0:T(8,128)(2,1)} %basis.3) | copy-start | bytes 147460
  42.4 29.9 %copy-start.7 = (bf16[1,1,64,64]{3,2,1,0:T(8,128)(2,1)S(1)}, bf16[1,1,64,64]{3,2,1,0:T(8,128)(2,1)}, u32[]{:S(2)}) copy-start(bf16[1,1,64,64]{3,2,1,0:T(8,128)(2,1)} %transfer.3) | copy-start | bytes 24580
  42.4 29.9 %copy-start.10 = (s32[1,16]{1,0:T(1,128)S(1)}, s32[1,16]{1,0:T(1,128)}, u32[]{:S(2)}) copy-start(s32[1,16]{1,0:T(1,128)} %listing.1) | copy-start | bytes 196
  42.4 29.9 %all-to-all-start.1 = ((bf16[16,64,128]{2,1,0:T(8,128)(2,1)}), bf16[16,64,128]{2,1,0:T(8,128)(2,1)S(1)}, u32[]{:S(2)}, u32[]{:S(2)}) async-start(bf16[16,64,128]{2,1,0:T(8,128)(2,1)} %mid.1), calls=%async_computation.1 | async-start | bytes 524288 | tf_op jit(solution)/shard_map/all_to_all | solution.py:189
  49.9 12.6 %collective-permute-start.4 = (bf16[3,128,384]{2,1,0:T(8,128)(2,1)S(1)}, bf16[3,128,384]{2,1,0:T(8,128)(2,1)S(1)}, u32[]{:S(2)}, u32[]{:S(2)}) collective-permute-start(bf16[3,128,384]{2,1,0:T(8,128)(2,1)S(1)} %pad_maximum_fusion.here), channel_id=1, source_target_pairs={{32,0},{64,32},{96,64},{128,96},{160,128},{192,160},{224,192},{256... | collective-permute-start | bytes 884744 | tf_op jit(solution)/shard_map/ppermute | solution.py:15
  50.2 18.6 %collective-permute-start.5 = (bf16[3,128,384]{2,1,0:T(8,128)(2,1)S(1)}, bf16[3,128,384]{2,1,0:T(8,128)(2,1)S(1)}, u32[]{:S(2)}, u32[]{:S(2)}) collective-permute-start(bf16[3,128,384]{2,1,0:T(8,128)(2,1)S(1)} %pad_maximum_fusion.here), channel_id=1, source_target_pairs={{64,0},{96,32},{128,64},{160,96},{192,128},{224,160},{256,192},{28... | collective-permute-start | bytes 884744 | tf_op jit(solution)/shard_map/ppermute | solution.py:15
  68.8 1.8 %copy-start.1 = (bf16[1,1,9,384,384]{4,3,2,1,0:T(8,128)(2,1)S(1)}, bf16[1,1,9,384,384]{4,3,2,1,0:T(8,128)(2,1)}, u32[]{:S(2)}) copy-start(bf16[1,1,9,384,384]{4,3,2,1,0:T(8,128)(2,1)} %blocks.1) | copy-start | bytes 7962628

commit v2 on v1

--- a/solution.py
+++ b/solution.py
@@ -7,6 +7,8 @@
 
 VMEM = pltpu.VMEM
 SMEM = pltpu.SMEM
+VL = 8
+LINES = 8
 HALF_BAND = 15
 
 
@@ -36,6 +38,20 @@
         out[i] = chunk
 
 
+def fold_kernel(gathered, out):
+    lines, depth = gathered.shape[0], gathered.shape[1]
+    rank = 2 * depth // 3
+    half = rank // 2
+    low = gathered[:, :half].reshape(lines * half, -1)
+    high = gathered[:, half:rank].reshape(lines * half, -1)
+    packed = gathered[:, rank:].reshape(lines * half, -1)
+    region = contract_rows(packed[:, :rank], low) + contract_rows(packed[:, rank:], high)
+    leaves = gathered[:, :rank].reshape(lines * rank, -1)
+    chunk = jnp.concatenate([leaves, region.astype(out.dtype)], axis=0)
+    for i in range(out.shape[0]):
+        out[i] = chunk
+
+
 def pack_kernel(first, second, out_first, out_second):
     for source, out in ((first, out_first), (second, out_second)):
         bands, rank = source.shape[3], source.shape[4]
@@ -47,17 +63,14 @@
 
 def mid_kernel(place, gathered, own, first, second, out, turned):
     row, col = place[0], place[1]
-    cols, rank = gathered.shape[0], own.shape[4]
-    rows = out.shape[0]
-    bands = own.shape[3]
+    bands, rank = own.shape[3], own.shape[4]
+    groups, lines = gathered.shape[0], gathered.shape[1] // rank - 1
+    cols, rows = groups * lines, out.shape[0]
     for j in range(cols):
-        turned[j * rank : (j + 1) * rank] = gathered[lax.rem(col + 3 + j, cols), :rank]
-    half = rank // 2
-    low = gathered[:, :half].reshape(cols * half, -1)
-    high = gathered[:, half:rank].reshape(cols * half, -1)
-    packed = gathered[:, rank:].reshape(cols * half, -1)
-    region = contract_rows(packed[:, :rank], low) + contract_rows(packed[:, rank:], high)
-    region = region.astype(out.dtype)
+        source = lax.rem(col + 3 + j, cols)
+        start = pl.multiple_of(lax.rem(source, lines) * rank, rank)
+        turned[j * rank : (j + 1) * rank] = gathered[source // lines, pl.ds(start, rank)]
+    region = sum(gathered[x, lines * rank :].astype(jnp.float32) for x in range(groups)).astype(out.dtype)
     for a in range(rows):
         out[a] = region
     out[row] = contract_rows(own[0, 0, 0].reshape(bands * rank, rank), turned[: bands * rank]).astype(out.dtype)
@@ -102,6 +115,10 @@
     out[0, 0] = (near[...] + far).astype(out.dtype)
 
 
+def whole(shape):
+    return pl.BlockSpec(shape, lambda i: (0,) * len(shape))
+
+
 def call(kernel, out_shape, in_specs, scratch, cost, name):
     return pl.pallas_call(
         kernel,
@@ -110,7 +127,7 @@
         out_specs=jax.tree.map(lambda _: pl.BlockSpec(memory_space=VMEM), out_shape),
         scratch_shapes=scratch,
         cost_estimate=pl.CostEstimate(flops=cost[0], bytes_accessed=cost[1], transcendentals=0),
-        compiler_params=pltpu.CompilerParams(vmem_limit_bytes=24 * 1024 * 1024),
+        compiler_params=pltpu.CompilerParams(vmem_limit_bytes=VL * 1024 * 1024),
         name=name,
     )
 
@@ -139,21 +156,37 @@
     col_one = shifted(vectors[0, 0], "col", 1)
     col_two = shifted(vectors[0, 0], "col", 2)
 
-    chunks = call(
+    chunk_shape = (LINES, rank + rank // 2, vecs)
+    groups = cols // LINES
+    chunks = pl.pallas_call(
         leaf_kernel,
-        jax.ShapeDtypeStruct((cols, rank + rank // 2, vecs), bf16),
-        [vmem] * 3,
-        [],
-        (2 * rank * vecs * leaf, 2 * cols * 96 * vecs),
-        "leaf",
+        grid=(1,),
+        out_shape=jax.ShapeDtypeStruct(chunk_shape, bf16),
+        in_specs=[whole(a.shape) for a in (vectors, basis_col, transfer_col)],
+        out_specs=whole(chunk_shape),
+        cost_estimate=pl.CostEstimate(flops=2 * rank * vecs * leaf, bytes_accessed=1000000, transcendentals=0),
+        name="leaf",
     )(vectors, basis_col, transfer_col)
-    gathered = lax.all_to_all(chunks, "col", split_axis=0, concat_axis=0, tiled=True)
+    near_cols = [[x * LINES + z for z in range(LINES)] for x in range(groups)]
+    far_cols = [[x * LINES + z for x in range(groups)] for z in range(LINES)]
+    line = lax.all_to_all(chunks, "col", 0, 0, axis_index_groups=near_cols, tiled=True)
+    folded_shape = (groups, (LINES + 1) * rank, vecs)
+    folded = pl.pallas_call(
+        fold_kernel,
+        grid=(1,),
+        out_shape=jax.ShapeDtypeStruct(folded_shape, bf16),
+        in_specs=[whole(chunk_shape)],
+        out_specs=whole(folded_shape),
+        cost_estimate=pl.CostEstimate(flops=2 * LINES * rank * rank * vecs, bytes_accessed=1000000, transcendentals=0),
+        name="fold",
+    )(line)
+    gathered = lax.all_to_all(folded, "col", 0, 0, axis_index_groups=far_cols, tiled=True)
 
     def slab(d):
         return pl.BlockSpec((1, 1, 1, bands, rank, rank), lambda i: (0, 0, d, 0, 0, 0))
 
     packed_shape = jax.ShapeDtypeStruct((HALF_BAND * rank, 2 * rank), bf16)
-    first, second = pl.pallas_call(
+    packed_one, packed_two = pl.pallas_call(
         pack_kernel,
         grid=(1,),
         out_shape=[packed_shape] * 2,
@@ -162,20 +195,22 @@
         cost_estimate=pl.CostEstimate(flops=0, bytes_accessed=2000000, transcendentals=0),
         name="pack",
     )(leaf_couple, leaf_couple)
-    first = shifted(first, "row", -1)
-    second = shifted(second, "row", -2)
-
+    first = shifted(packed_one, "row", -1)
+    second = shifted(packed_two, "row", -2)
+
+    col_one, first, second = lax.optimization_barrier((col_one, first, second))
     here = jnp.stack([vectors[0, 0], col_one, col_two])
     row_one = shifted(here, "row", 1)
     row_two = shifted(here, "row", 2)
 
+    leaf_couple, here = lax.optimization_barrier((leaf_couple, here))
     outgoing = pl.pallas_call(
         mid_kernel,
         grid=(1,),
         out_shape=jax.ShapeDtypeStruct((rows, rank, vecs), bf16),
         in_specs=[
             smem,
-            pl.BlockSpec((cols, rank + rank // 2, vecs), lambda i: (0, 0, 0)),
+            whole(folded_shape),
             slab(0),
             pl.BlockSpec(packed_shape.shape, lambda i: (0, 0)),
             pl.BlockSpec(packed_shape.shape, lambda i: (0, 0)),
@@ -183,7 +218,7 @@
         out_specs=pl.BlockSpec((rows, rank, vecs), lambda i: (0, 0, 0)),
         scratch_shapes=[VMEM((cols * rank, vecs), bf16)],
         cost_estimate=pl.CostEstimate(flops=2 * 2048 * 256 * 128, bytes_accessed=3000000, transcendentals=0),
-        compiler_params=pltpu.CompilerParams(vmem_limit_bytes=24 * 1024 * 1024),
+        compiler_params=pltpu.CompilerParams(vmem_limit_bytes=VL * 1024 * 1024),
         name="mid",
     )(place, gathered, leaf_couple, first, second)
     received = lax.all_to_all(outgoing, "row", split_axis=0, concat_axis=0, tiled=True)
@@ -193,7 +228,7 @@
         jax.ShapeDtypeStruct((vecs, leaf), f32),
         [smem, smem, vmem, vmem, vmem, vmem],
         [SMEM((near_blocks.shape[2],), jnp.int32)],
-        (2 * 9 * vecs * leaf * leaf, 2 * 9 * leaf * (leaf + vecs)),
+        (2**36, 2 * 9 * leaf * (leaf + vecs)),
         "near",
     )(near_source, near_count, near_blocks, here, row_one, row_two)
 

time: 74.7 us -> 70.2 us (0.940)
  the two profiles are of different devices: /device:TPU:24 before, /device:TPU:1 now
where the time goes in v2:
time: 70.2 us; the launch traced here: 69.7 us
  starting transfers between devices  40 us (57%)
  waiting for transfers between devices  14.8 us (21%)
  Pallas kernels  11.4 us (16%)
  local copies, waits for them, and re-layouts  2.51 us (4%)
  between operations  0.86 us (1%)
    ppermute x6, starting transfers between devices, shifted(): lax.ppermute(value, axis, [((i + steps) % count, i) for i in range(count)])  19.7 us
    all_to_all x1, starting transfers between devices, per_device(): lax.all_to_all(chunks, 'col', 0, 0, axis_index_groups=near_cols, tiled=True)  10.9 us
    all_to_all x1, waiting for transfers between devices, per_device(): lax.all_to_all(outgoing, 'row', split_axis=0, concat_axis=0, tiled=True)  8.37 us
    all_to_all x1, waiting for transfers between devices, per_device(): lax.all_to_all(folded, 'col', 0, 0, axis_index_groups=far_cols, tiled=True)  6.42 us
    all_to_all x1, starting transfers between devices, per_device(): lax.all_to_all(outgoing, 'row', split_axis=0, concat_axis=0, tiled=True)  5.84 us
    all_to_all x1, starting transfers between devices, per_device(): lax.all_to_all(folded, 'col', 0, 0, axis_index_groups=far_cols, tiled=True)  3.61 us
    unnamed x18, local copies, waits for them, and re-layouts  2.51 us
    pallas_call x1, Pallas kernels, per_device(): pl.pallas_call(pack_kernel, grid=(1,), out_shape=[packed_shape] * 2, in_s...  2.19 us
  transfers between devices with their start and end apart: 9, of which 2 were waited for; matrix products, arithmetic and copies ran while one was open for 0% of the time, Pallas kernels for 11%

profile of v2, /device:TPU:1, one launch (start us, length us, event | category | flops | bytes accessed | tf_op | source)
XLA Modules:
  0.0 69.7 jit_solution(10855312473454369859)
XLA Ops:
  0.0 1.8 %leaf.1 = bf16[8,96,128]{2,1,0:T(8,128)(2,1)} custom-call(bf16[1,1,128,384]{3,2,1,0:T(8,128)(2,1)} %vectors.1, bf16[1,1,64,384]{3,2,1,0:T(8,128)(2,1)} %basis.2, bf16[1,1,64,64]{3,2,1,0:T(8,128)(2,1)} %transfer.2), custom_call_target="tpu_custom_call" | custom-call | flops 6291456 | bytes 1000000 | tf_op jit(solution)/shard_map/leaf/pallas_call | solution.py:161
  1.8 10.9 %all-to-all-start = ((bf16[8,96,128]{2,1,0:T(8,128)(2,1)}), bf16[8,96,128]{2,1,0:T(8,128)(2,1)S(1)}, u32[]{:S(2)}, u32[]{:S(2)}) async-start(bf16[8,96,128]{2,1,0:T(8,128)(2,1)} %leaf.1), calls=%async_computation | async-start | bytes 393216 | tf_op jit(solution)/shard_map/all_to_all | solution.py:172
  12.7 2.2 %pack.1 = (bf16[960,128]{1,0:T(8,128)(2,1)}, bf16[960,128]{1,0:T(8,128)(2,1)}) custom-call(bf16[1,1,3,29,64,64]{5,4,3,2,1,0:T(8,128)(2,1)} %own, bf16[1,1,3,29,64,64]{5,4,3,2,1,0:T(8,128)(2,1)} %own), custom_call_target="tpu_custom_call" | custom-call | bytes 2000000 | tf_op jit(solution)/shard_map/pack/pallas_call | solution.py:189
  14.9 2.1 %collective-permute-start.1 = (bf16[960,128]{1,0:T(8,128)(2,1)}, bf16[960,128]{1,0:T(8,128)(2,1)S(1)}, u32[]{:S(2)}, u32[]{:S(2)}) collective-permute-start(bf16[960,128]{1,0:T(8,128)(2,1)} %get-tuple-element.12), channel_id=1, source_target_pairs={{480,0},{0,32},{32,64},{64,96},{96,128},{128,160},{160,192},{192,2... | collective-permute-start | bytes 737288 | tf_op jit(solution)/shard_map/ppermute | solution.py:17
  17.0 3.2 %collective-permute-start.2 = (bf16[960,128]{1,0:T(8,128)(2,1)}, bf16[960,128]{1,0:T(8,128)(2,1)S(1)}, u32[]{:S(2)}, u32[]{:S(2)}) collective-permute-start(bf16[960,128]{1,0:T(8,128)(2,1)} %get-tuple-element.13), channel_id=1, source_target_pairs={{448,0},{480,32},{0,64},{32,96},{64,128},{96,160},{128,192},{160,2... | collective-permute-start | bytes 737288 | tf_op jit(solution)/shard_map/ppermute | solution.py:17
  20.2 7.0 %collective-permute-start = (bf16[128,384]{1,0:T(8,128)(2,1)S(1)}, bf16[128,384]{1,0:T(8,128)(2,1)S(1)}, u32[]{:S(2)}, u32[]{:S(2)}) collective-permute-start(bf16[128,384]{1,0:T(8,128)(2,1)S(1)} %bitcast.6), channel_id=1, source_target_pairs={{1,0},{2,1},{3,2},{4,3},{5,4},{6,5},{7,6},{8,7},{9,8},{10,9},{11,1... | collective-permute-start | bytes 294920 | tf_op jit(solution)/shard_map/ppermute | solution.py:17
  27.3 4.0 %collective-permute-start.3 = (bf16[128,384]{1,0:T(8,128)(2,1)S(1)}, bf16[128,384]{1,0:T(8,128)(2,1)S(1)}, u32[]{:S(2)}, u32[]{:S(2)}) collective-permute-start(bf16[128,384]{1,0:T(8,128)(2,1)S(1)} %bitcast.7), channel_id=1, source_target_pairs={{2,0},{3,1},{4,2},{5,3},{6,4},{7,5},{8,6},{9,7},{10,8},{11,9},{12,... | collective-permute-start | bytes 294920 | tf_op jit(solution)/shard_map/ppermute | solution.py:17
  31.3 0.7 copy-done.7
  32.0 2.0 %fold.1 = bf16[4,576,128]{2,1,0:T(8,128)(2,1)} custom-call(bf16[8,96,128]{2,1,0:T(8,128)(2,1)} %copy-done.7), custom_call_target="tpu_custom_call" | custom-call | flops 8388608 | bytes 1000000 | tf_op jit(solution)/shard_map/fold/pallas_call | solution.py:174
  34.0 3.6 %all-to-all-start.1 = ((bf16[4,576,128]{2,1,0:T(8,128)(2,1)}), bf16[4,576,128]{2,1,0:T(8,128)(2,1)S(1)}, u32[]{:S(2)}, u32[]{:S(2)}) async-start(bf16[4,576,128]{2,1,0:T(8,128)(2,1)} %fold.1), calls=%async_computation.1 | async-start | bytes 1179648 | tf_op jit(solution)/shard_map/all_to_all | solution.py:183
  37.7 0.0 collective-permute-start.4
  37.7 3.3 %collective-permute-start.5 = (bf16[3,128,384]{2,1,0:T(8,128)(2,1)S(1)}, bf16[3,128,384]{2,1,0:T(8,128)(2,1)S(1)}, u32[]{:S(2)}, u32[]{:S(2)}) collective-permute-start(bf16[3,128,384]{2,1,0:T(8,128)(2,1)S(1)} %pad_maximum_fusion.here), channel_id=1, source_target_pairs={{64,0},{96,32},{128,64},{160,96},{192,128},{224,160},{256,192},{28... | collective-permute-start | bytes 884744 | tf_op jit(solution)/shard_map/ppermute | solution.py:17
  41.7 0.1 pad_add_fusion.place
  41.8 6.4 %all-to-all-done.1.gathered = bf16[4,576,128]{2,1,0:T(8,128)(2,1)S(1)} async-done(((bf16[4,576,128]{2,1,0:T(8,128)(2,1)}), bf16[4,576,128]{2,1,0:T(8,128)(2,1)S(1)}, u32[]{:S(2)}, u32[]{:S(2)}) %all-to-all-start.1) | async-done | bytes 589856 | tf_op jit(solution)/shard_map/all_to_all | solution.py:183
  48.2 2.1 %mid.1 = bf16[16,64,128]{2,1,0:T(8,128)(2,1)} custom-call(s32[2]{0:T(128)S(1)} %pad_add_fusion.place, bf16[4,576,128]{2,1,0:T(8,128)(2,1)S(1)} %all-to-all-done.1.gathered, bf16[1,1,3,29,64,64]{5,4,3,2,1,0:T(8,128)(2,1)S(1)} %copy-done, bf16[960,128]{1,0:T(8,128)(2,1)S(1)} %collective-permute-done.1.first, bf16[960,128]{1,0:T(8,128)(2,1)S(1)} %collective-permute-done.2.second), custom_call_target="tpu_custom_call" | custom-call | flops 134217728 | bytes 3000000 | tf_op jit(solution)/shard_map/mid/pallas_call | solution.py:207
  50.2 5.8 %all-to-all-start.2 = ((bf16[16,64,128]{2,1,0:T(8,128)(2,1)}), bf16[16,64,128]{2,1,0:T(8,128)(2,1)S(1)}, u32[]{:S(2)}, u32[]{:S(2)}) async-start(bf16[16,64,128]{2,1,0:T(8,128)(2,1)} %mid.1), calls=%async_computation.2 | async-start | bytes 524288 | tf_op jit(solution)/shard_map/all_to_all | solution.py:224
  56.1 0.0 copy-start.2
  56.1 0.0 copy-start.3
  56.1 0.0 copy-start.4
  56.2 0.0 copy-start.5
  56.2 1.8 %copy-done.5 = bf16[1,1,9,384,384]{4,3,2,1,0:T(8,128)(2,1)S(1)} copy-done((bf16[1,1,9,384,384]{4,3,2,1,0:T(8,128)(2,1)S(1)}, bf16[1,1,9,384,384]{4,3,2,1,0:T(8,128)(2,1)}, u32[]{:S(2)}) %copy-start.5) | copy-done | bytes 2654232
  58.0 1.4 %near.1 = f32[128,384]{1,0:T(8,128)S(1)} custom-call(s32[1,1,9]{2,1,0:T(1,128)S(1)} %copy-done.6, s32[1,1]{1,0:T(1,128)S(6)} %copy.12.count, bf16[1,1,9,384,384]{4,3,2,1,0:T(8,128)(2,1)S(1)} %copy-done.5, bf16[3,128,384]{2,1,0:T(8,128)(2,1)S(1)} %pad_maximum_fusion.here, bf16[3,128,384]{2,1,0:T(8,128)(2,1)S(1)} %collective-permute-done.4.one, ...), custom_call_target="tpu_custom_call" | custom-call | flops 68719476736 | bytes 3538944 | tf_op jit(solution)/shard_map/near/pallas_call | solution.py:226
  59.4 8.4 %all-to-all-done.2.received = bf16[16,64,128]{2,1,0:T(8,128)(2,1)S(1)} async-done(((bf16[16,64,128]{2,1,0:T(8,128)(2,1)}), bf16[16,64,128]{2,1,0:T(8,128)(2,1)S(1)}, u32[]{:S(2)}, u32[]{:S(2)}) %all-to-all-start.2) | async-done | bytes 262176 | tf_op jit(solution)/shard_map/all_to_all | solution.py:224
  67.8 1.9 %final.1 = bf16[1,1,128,384]{3,2,1,0:T(8,128)(2,1)} custom-call(s32[2]{0:T(128)S(1)} %pad_add_fusion.place, s32[1,16]{1,0:T(1,128)S(1)} %copy-done.4, bf16[16,64,128]{2,1,0:T(8,128)(2,1)S(1)} %all-to-all-done.2.received, bf16[1,16,64,64]{3,2,1,0:T(8,128)(2,1)S(1)} %copy-done.1, bf16[1,1,64,64]{3,2,1,0:T(8,128)(2,1)S(1)} %copy-done.3, ...), custom_call_target="tpu_custom_call" | custom-call | flops 29360128 | bytes 1000000 | tf_op jit(solution)/shard_map/final/pallas_call | solution.py:235
  (20 shorter events, 0.1 us)
Async XLA Ops:
  0.0 20.2 %copy-start.8 = (bf16[1,1,128,384]{3,2,1,0:T(8,128)(2,1)S(1)}, bf16[1,1,128,384]{3,2,1,0:T(8,128)(2,1)}, u32[]{:S(2)}) copy-start(bf16[1,1,128,384]{3,2,1,0:T(8,128)(2,1)} %vectors.1) | copy-start | bytes 294916
  1.8 29.5 %all-to-all-start = ((bf16[8,96,128]{2,1,0:T(8,128)(2,1)}), bf16[8,96,128]{2,1,0:T(8,128)(2,1)S(1)}, u32[]{:S(2)}, u32[]{:S(2)}) async-start(bf16[8,96,128]{2,1,0:T(8,128)(2,1)} %leaf.1), calls=%async_computation | async-start | bytes 393216 | tf_op jit(solution)/shard_map/all_to_all | solution.py:172
  12.7 35.5 %copy-start = (bf16[1,1,3,29,64,64]{5,4,3,2,1,0:T(8,128)(2,1)S(1)}, bf16[1,1,3,29,64,64]{5,4,3,2,1,0:T(8,128)(2,1)}, u32[]{:S(2)}) copy-start(bf16[1,1,3,29,64,64]{5,4,3,2,1,0:T(8,128)(2,1)} %own) | copy-start | bytes 2138116
  14.9 22.7 %collective-permute-start.1 = (bf16[960,128]{1,0:T(8,128)(2,1)}, bf16[960,128]{1,0:T(8,128)(2,1)S(1)}, u32[]{:S(2)}, u32[]{:S(2)}) collective-permute-start(bf16[960,128]{1,0:T(8,128)(2,1)} %get-tuple-element.12), channel_id=1, source_target_pairs={{480,0},{0,32},{32,64},{64,96},{96,128},{128,160},{160,192},{192,2... | collective-permute-start | bytes 737288 | tf_op jit(solution)/shard_map/ppermute | solution.py:17
  17.0 20.6 %collective-permute-start.2 = (bf16[960,128]{1,0:T(8,128)(2,1)}, bf16[960,128]{1,0:T(8,128)(2,1)S(1)}, u32[]{:S(2)}, u32[]{:S(2)}) collective-permute-start(bf16[960,128]{1,0:T(8,128)(2,1)} %get-tuple-element.13), channel_id=1, source_target_pairs={{448,0},{480,32},{0,64},{32,96},{64,128},{96,160},{128,192},{160,2... | collective-permute-start | bytes 737288 | tf_op jit(solution)/shard_map/ppermute | solution.py:17
  20.2 17.4 %collective-permute-start = (bf16[128,384]{1,0:T(8,128)(2,1)S(1)}, bf16[128,384]{1,0:T(8,128)(2,1)S(1)}, u32[]{:S(2)}, u32[]{:S(2)}) collective-permute-start(bf16[128,384]{1,0:T(8,128)(2,1)S(1)} %bitcast.6), channel_id=1, source_target_pairs={{1,0},{2,1},{3,2},{4,3},{5,4},{6,5},{7,6},{8,7},{9,8},{10,9},{11,1... | collective-permute-start | bytes 294920 | tf_op jit(solution)/shard_map/ppermute | solution.py:17
  27.3 10.4 %collective-permute-start.3 = (bf16[128,384]{1,0:T(8,128)(2,1)S(1)}, bf16[128,384]{1,0:T(8,128)(2,1)S(1)}, u32[]{:S(2)}, u32[]{:S(2)}) collective-permute-start(bf16[128,384]{1,0:T(8,128)(2,1)S(1)} %bitcast.7), channel_id=1, source_target_pairs={{2,0},{3,1},{4,2},{5,3},{6,4},{7,5},{8,6},{9,7},{10,8},{11,9},{12,... | collective-permute-start | bytes 294920 | tf_op jit(solution)/shard_map/ppermute | solution.py:17
  31.3 0.7 copy-start.7
  34.0 22.2 %copy-start.6 = (s32[1,1,9]{2,1,0:T(1,128)S(1)}, s32[1,1,9]{2,1,0:T(1,128)}, u32[]{:S(2)}) copy-start(s32[1,1,9]{2,1,0:T(1,128)} %source.1) | copy-start | bytes 112
  34.0 14.2 %all-to-all-start.1 = ((bf16[4,576,128]{2,1,0:T(8,128)(2,1)}), bf16[4,576,128]{2,1,0:T(8,128)(2,1)S(1)}, u32[]{:S(2)}, u32[]{:S(2)}) async-start(bf16[4,576,128]{2,1,0:T(8,128)(2,1)} %fold.1), calls=%async_computation.1 | async-start | bytes 1179648 | tf_op jit(solution)/shard_map/all_to_all | solution.py:183
  37.7 18.4 %collective-permute-start.4 = (bf16[3,128,384]{2,1,0:T(8,128)(2,1)S(1)}, bf16[3,128,384]{2,1,0:T(8,128)(2,1)S(1)}, u32[]{:S(2)}, u32[]{:S(2)}) collective-permute-start(bf16[3,128,384]{2,1,0:T(8,128)(2,1)S(1)} %pad_maximum_fusion.here), channel_id=1, source_target_pairs={{32,0},{64,32},{96,64},{128,96},{160,128},{192,160},{224,192},{256... | collective-permute-start | bytes 884744 | tf_op jit(solution)/shard_map/ppermute | solution.py:17
  37.7 18.4 %collective-permute-start.5 = (bf16[3,128,384]{2,1,0:T(8,128)(2,1)S(1)}, bf16[3,128,384]{2,1,0:T(8,128)(2,1)S(1)}, u32[]{:S(2)}, u32[]{:S(2)}) collective-permute-start(bf16[3,128,384]{2,1,0:T(8,128)(2,1)S(1)} %pad_maximum_fusion.here), channel_id=1, source_target_pairs={{64,0},{96,32},{128,64},{160,96},{192,128},{224,160},{256,192},{28... | collective-permute-start | bytes 884744 | tf_op jit(solution)/shard_map/ppermute | solution.py:17
  50.2 17.6 %all-to-all-start.2 = ((bf16[16,64,128]{2,1,0:T(8,128)(2,1)}), bf16[16,64,128]{2,1,0:T(8,128)(2,1)S(1)}, u32[]{:S(2)}, u32[]{:S(2)}) async-start(bf16[16,64,128]{2,1,0:T(8,128)(2,1)} %mid.1), calls=%async_computation.2 | async-start | bytes 524288 | tf_op jit(solution)/shard_map/all_to_all | solution.py:224
  56.1 11.7 %copy-start.1 = (bf16[1,16,64,64]{3,2,1,0:T(8,128)(2,1)S(1)}, bf16[1,16,64,64]{3,2,1,0:T(8,128)(2,1)}, u32[]{:S(2)}) copy-start(bf16[1,16,64,64]{3,2,1,0:T(8,128)(2,1)} %coupling.1) | copy-start | bytes 393220
  56.1 11.7 %copy-start.2 = (bf16[1,1,64,384]{3,2,1,0:T(8,128)(2,1)S(1)}, bf16[1,1,64,384]{3,2,1,0:T(8,128)(2,1)}, u32[]{:S(2)}) copy-start(bf16[1,1,64,384]{3,2,1,0:T(8,128)(2,1)} %basis.3) | copy-start | bytes 147460
  56.1 11.7 %copy-start.3 = (bf16[1,1,64,64]{3,2,1,0:T(8,128)(2,1)S(1)}, bf16[1,1,64,64]{3,2,1,0:T(8,128)(2,1)}, u32[]{:S(2)}) copy-start(bf16[1,1,64,64]{3,2,1,0:T(8,128)(2,1)} %transfer.3) | copy-start | bytes 24580
  56.1 11.7 %copy-start.4 = (s32[1,16]{1,0:T(1,128)S(1)}, s32[1,16]{1,0:T(1,128)}, u32[]{:S(2)}) copy-start(s32[1,16]{1,0:T(1,128)} %listing.1) | copy-start | bytes 196
  56.2 1.8 %copy-start.5 = (bf16[1,1,9,384,384]{4,3,2,1,0:T(8,128)(2,1)S(1)}, bf16[1,1,9,384,384]{4,3,2,1,0:T(8,128)(2,1)}, u32[]{:S(2)}) copy-start(bf16[1,1,9,384,384]{4,3,2,1,0:T(8,128)(2,1)} %blocks.1) | copy-start | bytes 7962628

commit v3 on v2

--- a/solution.py
+++ b/solution.py
@@ -52,17 +52,18 @@
         out[i] = chunk
 
 
-def pack_kernel(first, second, out_first, out_second):
-    for source, out in ((first, out_first), (second, out_second)):
-        bands, rank = source.shape[3], source.shape[4]
-        left = source[0, 0, 0, :HALF_BAND].reshape(HALF_BAND * rank, rank)
-        right = source[0, 0, 0, HALF_BAND:].reshape((bands - HALF_BAND) * rank, rank)
-        right = jnp.concatenate([right, jnp.zeros(((2 * HALF_BAND - bands) * rank, rank), right.dtype)], axis=0)
-        out[...] = jnp.concatenate([left, right], axis=1)
-
-
-def mid_kernel(place, gathered, own, first, second, out, turned):
-    row, col = place[0], place[1]
+def pack_kernel(couple, out_first, out_second):
+    bands, rank = couple.shape[3], couple.shape[4]
+    size = HALF_BAND * rank
+    rest = (bands - HALF_BAND) * rank
+    for d, out in ((1, out_first), (2, out_second)):
+        out[:, :rank] = couple[0, 0, d, :HALF_BAND].reshape(size, rank)
+        out[:rest, rank:] = couple[0, 0, d, HALF_BAND:].reshape(rest, rank)
+        out[rest:, rank:] = jnp.zeros((size - rest, rank), out.dtype)
+
+
+def mid_kernel(gathered, own, first, second, out, turned):
+    row, col = lax.axis_index("row"), lax.axis_index("col")
     bands, rank = own.shape[3], own.shape[4]
     groups, lines = gathered.shape[0], gathered.shape[1] // rank - 1
     cols, rows = groups * lines, out.shape[0]
@@ -75,15 +76,23 @@
         out[a] = region
     out[row] = contract_rows(own[0, 0, 0].reshape(bands * rank, rank), turned[: bands * rank]).astype(out.dtype)
     size = HALF_BAND * rank
-    for d, weights in ((1, first), (2, second)):
-        term = contract_rows(weights[:, :rank], turned[:size]) + contract_rows(
-            weights[:, rank:], turned[size : 2 * size]
-        )
+    both = jnp.concatenate([first[...], second[...]], axis=1)
+    low = contract_rows(both, turned[:size])
+    high = contract_rows(both, turned[size : 2 * size])
+    for d in (1, 2):
+        start = 2 * (d - 1) * rank
+        term = low[start : start + rank] + high[start + rank : start + 2 * rank]
         out[lax.rem(row + rows - d, rows)] = term.astype(out.dtype)
 
 
-def near_kernel(source, count, blocks, here, one, two, out, slot_of):
+def near_kernel(source, count, listing, blocks, here, one, two, coupling, out, ordered, slot_of):
     slots = blocks.shape[2]
+    rows = coupling.shape[1]
+    row = lax.axis_index("row")
+    for f in range(rows):
+        region = listing[0, f]
+        is_far = lax.rem(region - row + rows, rows) >= 3
+        ordered[region] = jnp.where(is_far, coupling[0, f], jnp.zeros_like(coupling[0, f]))
     for s in range(slots):
         slot_of[source[0, 0, s]] = s
     live_count = count[0, 0]
@@ -97,17 +106,15 @@
             out[...] += jnp.dot(bundle[cell % 3], blocks[0, 0, slot], preferred_element_type=jnp.float32)
 
 
-def final_kernel(place, listing, received, coupling, transfer, basis, near, out, terms):
-    row = place[0]
+def final_kernel(received, ordered, transfer, basis, near, out):
+    row = lax.axis_index("row")
     rows, rank = received.shape[0], received.shape[1]
-    band = jnp.zeros(received.shape[1:], jnp.float32)
-    for f in range(rows):
-        region = listing[0, f]
-        part = received[region]
-        is_far = lax.rem(region - row + rows, rows) >= 3
-        terms[f * rank : (f + 1) * rank] = jnp.where(is_far, part, jnp.zeros_like(part))
-        band += jnp.where(is_far, jnp.zeros_like(part), part).astype(jnp.float32)
-    outgoing = contract_rows(coupling[0].reshape(rows * rank, rank), terms[...])
+    band = received[row].astype(jnp.float32)
+    for d in (1, 2):
+        band += received[lax.rem(row + d, rows)].astype(jnp.float32)
+    outgoing = contract_rows(
+        ordered[...].reshape(rows * rank, rank), received[...].reshape(rows * rank, received.shape[2])
+    )
     leaf_out = band + exact_rows(transfer[0, 0], outgoing)
     high = leaf_out.astype(jnp.bfloat16)
     low = (leaf_out - high.astype(jnp.float32)).astype(jnp.bfloat16)
@@ -151,7 +158,6 @@
     bands = leaf_couple.shape[3]
     bf16, f32 = jnp.bfloat16, jnp.float32
     vmem, smem = pl.BlockSpec(memory_space=VMEM), pl.BlockSpec(memory_space=SMEM)
-    place = jnp.stack([lax.axis_index("row"), lax.axis_index("col")]).astype(jnp.int32)
 
     col_one = shifted(vectors[0, 0], "col", 1)
     col_two = shifted(vectors[0, 0], "col", 2)
@@ -171,75 +177,61 @@
     far_cols = [[x * LINES + z for x in range(groups)] for z in range(LINES)]
     line = lax.all_to_all(chunks, "col", 0, 0, axis_index_groups=near_cols, tiled=True)
     folded_shape = (groups, (LINES + 1) * rank, vecs)
-    folded = pl.pallas_call(
+    folded = call(
         fold_kernel,
-        grid=(1,),
-        out_shape=jax.ShapeDtypeStruct(folded_shape, bf16),
-        in_specs=[whole(chunk_shape)],
-        out_specs=whole(folded_shape),
-        cost_estimate=pl.CostEstimate(flops=2 * LINES * rank * rank * vecs, bytes_accessed=1000000, transcendentals=0),
-        name="fold",
+        jax.ShapeDtypeStruct(folded_shape, bf16),
+        [vmem],
+        [],
+        (2 * LINES * rank * rank * vecs, 1000000),
+        "fold",
     )(line)
     gathered = lax.all_to_all(folded, "col", 0, 0, axis_index_groups=far_cols, tiled=True)
 
-    def slab(d):
-        return pl.BlockSpec((1, 1, 1, bands, rank, rank), lambda i: (0, 0, d, 0, 0, 0))
-
     packed_shape = jax.ShapeDtypeStruct((HALF_BAND * rank, 2 * rank), bf16)
-    packed_one, packed_two = pl.pallas_call(
+    packed_one, packed_two = call(
         pack_kernel,
-        grid=(1,),
-        out_shape=[packed_shape] * 2,
-        in_specs=[slab(1), slab(2)],
-        out_specs=[pl.BlockSpec(packed_shape.shape, lambda i: (0, 0))] * 2,
-        cost_estimate=pl.CostEstimate(flops=0, bytes_accessed=2000000, transcendentals=0),
-        name="pack",
-    )(leaf_couple, leaf_couple)
+        [packed_shape] * 2,
+        [vmem],
+        [],
+        (0, 2000000),
+        "pack",
+    )(leaf_couple)
+    col_one, col_two, packed_one, packed_two = lax.optimization_barrier((col_one, col_two, packed_one, packed_two))
     first = shifted(packed_one, "row", -1)
     second = shifted(packed_two, "row", -2)
 
-    col_one, first, second = lax.optimization_barrier((col_one, first, second))
     here = jnp.stack([vectors[0, 0], col_one, col_two])
     row_one = shifted(here, "row", 1)
     row_two = shifted(here, "row", 2)
 
     leaf_couple, here = lax.optimization_barrier((leaf_couple, here))
-    outgoing = pl.pallas_call(
+    outgoing = call(
         mid_kernel,
-        grid=(1,),
-        out_shape=jax.ShapeDtypeStruct((rows, rank, vecs), bf16),
-        in_specs=[
-            smem,
-            whole(folded_shape),
-            slab(0),
-            pl.BlockSpec(packed_shape.shape, lambda i: (0, 0)),
-            pl.BlockSpec(packed_shape.shape, lambda i: (0, 0)),
-        ],
-        out_specs=pl.BlockSpec((rows, rank, vecs), lambda i: (0, 0, 0)),
-        scratch_shapes=[VMEM((cols * rank, vecs), bf16)],
-        cost_estimate=pl.CostEstimate(flops=2 * 2048 * 256 * 128, bytes_accessed=3000000, transcendentals=0),
-        compiler_params=pltpu.CompilerParams(vmem_limit_bytes=VL * 1024 * 1024),
-        name="mid",
-    )(place, gathered, leaf_couple, first, second)
+        jax.ShapeDtypeStruct((rows, rank, vecs), bf16),
+        [vmem, vmem, vmem, vmem],
+        [VMEM((cols * rank, vecs), bf16)],
+        (2**29, 3000000),
+        "mid",
+    )(gathered, leaf_couple, first, second)
     received = lax.all_to_all(outgoing, "row", split_axis=0, concat_axis=0, tiled=True)
 
-    near = call(
+    near, ordered = call(
         near_kernel,
-        jax.ShapeDtypeStruct((vecs, leaf), f32),
-        [smem, smem, vmem, vmem, vmem, vmem],
+        [jax.ShapeDtypeStruct((vecs, leaf), f32), jax.ShapeDtypeStruct(coupling.shape[1:], bf16)],
+        [smem, smem, smem, vmem, vmem, vmem, vmem, vmem],
         [SMEM((near_blocks.shape[2],), jnp.int32)],
         (2**36, 2 * 9 * leaf * (leaf + vecs)),
         "near",
-    )(near_source, near_count, near_blocks, here, row_one, row_two)
+    )(near_source, near_count, distant_region_list, near_blocks, here, row_one, row_two, coupling)
 
     return call(
         final_kernel,
         jax.ShapeDtypeStruct((1, 1, vecs, leaf), bf16),
-        [smem, smem, vmem, vmem, vmem, vmem, vmem],
-        [VMEM((rows * rank, vecs), bf16)],
+        [vmem] * 5,
+        [],
         (2 * 1024 * 64 * 128 + 4 * 64 * 128 * 384, 1000000),
         "final",
-    )(place, distant_region_list, received, coupling, transfer_row, basis_row, near)
+    )(received, ordered, transfer_row, basis_row, near)
 
 
 def solution(mesh):

time: 70.2 us -> 64.3 us (0.916)
  waiting for transfers between devices: 14.8 us -> 10 us
  Pallas kernels: 11.4 us -> 7.96 us
  starting transfers between devices: 40 us -> 42.2 us
    all_to_all x1, waiting for transfers between devices: 6.42 us -> 0.01 us  [per_device(): lax.all_to_all(folded, 'col', 0, 0, axis_index_groups=far_cols, tiled=True)]
    pallas_call x5, Pallas kernels: 9.58 us -> 6.09 us  [the longest x1 1.99 us: per_device(): call(near_kernel, [jax.ShapeDtypeStruct((vecs, leaf), f32), jax.ShapeDtyp...]
    ppermute x6, waiting for transfers between devices: 0.02 us -> 3.09 us  [shifted(): lax.ppermute(value, axis, [((i + steps) % count, i) for i in range(count)])]
    all_to_all x1, starting transfers between devices: 5.84 us -> 7.62 us  [per_device(): lax.all_to_all(outgoing, 'row', split_axis=0, concat_axis=0, tiled=True)]
    all_to_all x1, waiting for transfers between devices: 8.37 us -> 6.95 us  [per_device(): lax.all_to_all(outgoing, 'row', split_axis=0, concat_axis=0, tiled=True)]
    unnamed x18 -> x16, local copies, waits for them, and re-layouts: 2.51 us -> 2.72 us
  transfers between devices with their start and end apart: 9 -> 9, of which waited for: 2 -> 2; matrix products, arithmetic and copies ran while one was open for 0% -> 0% of each run, Pallas kernels for 11% -> 8%
where the time goes in v3:
time: 64.3 us; the launch traced here: 63.8 us
  starting transfers between devices  42.2 us (66%)
  waiting for transfers between devices  10 us (16%)
  Pallas kernels  7.96 us (12%)
  local copies, waits for them, and re-layouts  2.72 us (4%)
  between operations  0.83 us (1%)
    ppermute x6, starting transfers between devices, shifted(): lax.ppermute(value, axis, [((i + steps) % count, i) for i in range(count)])  20.2 us
    all_to_all x1, starting transfers between devices, per_device(): lax.all_to_all(chunks, 'col', 0, 0, axis_index_groups=near_cols, tiled=True)  10.9 us
    all_to_all x1, starting transfers between devices, per_device(): lax.all_to_all(outgoing, 'row', split_axis=0, concat_axis=0, tiled=True)  7.62 us
    all_to_all x1, waiting for transfers between devices, per_device(): lax.all_to_all(outgoing, 'row', split_axis=0, concat_axis=0, tiled=True)  6.95 us
    all_to_all x1, starting transfers between devices, per_device(): lax.all_to_all(folded, 'col', 0, 0, axis_index_groups=far_cols, tiled=True)  3.48 us
    ppermute x6, waiting for transfers between devices, shifted(): lax.ppermute(value, axis, [((i + steps) % count, i) for i in range(count)])  3.09 us
    unnamed x16, local copies, waits for them, and re-layouts  2.72 us
    pallas_call x1, Pallas kernels, per_device(): call(near_kernel, [jax.ShapeDtypeStruct((vecs, leaf), f32), jax.ShapeDtyp...  1.99 us
  transfers between devices with their start and end apart: 9, of which 2 were waited for; matrix products, arithmetic and copies ran while one was open for 0% of the time, Pallas kernels for 8%

profile of v3, /device:TPU:1, one launch (start us, length us, event | category | flops | bytes accessed | tf_op | source)
XLA Modules:
  0.0 63.8 jit_solution(17937140978702013711)
XLA Ops:
  0.0 1.9 %leaf.1 = bf16[8,96,128]{2,1,0:T(8,128)(2,1)} custom-call(bf16[1,1,128,384]{3,2,1,0:T(8,128)(2,1)} %vectors.1, bf16[1,1,64,384]{3,2,1,0:T(8,128)(2,1)} %basis.2, bf16[1,1,64,64]{3,2,1,0:T(8,128)(2,1)} %transfer.2), custom_call_target="tpu_custom_call" | custom-call | flops 6291456 | bytes 1000000 | tf_op jit(solution)/shard_map/leaf/pallas_call | solution.py:167
  1.9 10.9 %all-to-all-start = ((bf16[8,96,128]{2,1,0:T(8,128)(2,1)}), bf16[8,96,128]{2,1,0:T(8,128)(2,1)S(1)}, u32[]{:S(2)}, u32[]{:S(2)}) async-start(bf16[8,96,128]{2,1,0:T(8,128)(2,1)} %leaf.1), calls=%async_computation | async-start | bytes 393216 | tf_op jit(solution)/shard_map/all_to_all | solution.py:178
  12.7 6.8 %collective-permute-start = (bf16[128,384]{1,0:T(8,128)(2,1)}, bf16[128,384]{1,0:T(8,128)(2,1)S(1)}, u32[]{:S(2)}, u32[]{:S(2)}) collective-permute-start(bf16[128,384]{1,0:T(8,128)(2,1)} %bitcast.4), channel_id=1, source_target_pairs={{1,0},{2,1},{3,2},{4,3},{5,4},{6,5},{7,6},{8,7},{9,8},{10,9},{11,1... | collective-permute-start | bytes 294920 | tf_op jit(solution)/shard_map/ppermute | solution.py:17
  19.5 4.0 %collective-permute-start.1 = (bf16[128,384]{1,0:T(8,128)(2,1)}, bf16[128,384]{1,0:T(8,128)(2,1)S(1)}, u32[]{:S(2)}, u32[]{:S(2)}) collective-permute-start(bf16[128,384]{1,0:T(8,128)(2,1)} %bitcast.5), channel_id=1, source_target_pairs={{2,0},{3,1},{4,2},{5,3},{6,4},{7,5},{8,6},{9,7},{10,8},{11,9},{12,... | collective-permute-start | bytes 294920 | tf_op jit(solution)/shard_map/ppermute | solution.py:17
  23.5 1.1 %fold.1 = bf16[4,576,128]{2,1,0:T(8,128)(2,1)} custom-call(bf16[8,96,128]{2,1,0:T(8,128)(2,1)S(1)} %all-to-all-done.gathered), custom_call_target="tpu_custom_call" | custom-call | flops 8388608 | bytes 1000000 | tf_op jit(solution)/shard_map/fold/pallas_call | solution.py:180
  24.6 3.5 %all-to-all-start.1 = ((bf16[4,576,128]{2,1,0:T(8,128)(2,1)}), bf16[4,576,128]{2,1,0:T(8,128)(2,1)S(1)}, u32[]{:S(2)}, u32[]{:S(2)}) async-start(bf16[4,576,128]{2,1,0:T(8,128)(2,1)} %fold.1), calls=%async_computation.1 | async-start | bytes 1179648 | tf_op jit(solution)/shard_map/all_to_all | solution.py:188
  28.1 0.0 copy-start.5
  28.1 0.0 copy-start.6
  28.1 0.3 pack.1
  28.4 0.0 collective-permute-done
  28.4 3.0 %collective-permute-start.2 = (bf16[960,128]{1,0:T(8,128)(2,1)S(1)}, bf16[960,128]{1,0:T(8,128)(2,1)S(1)}, u32[]{:S(2)}, u32[]{:S(2)}) collective-permute-start(bf16[960,128]{1,0:T(8,128)(2,1)S(1)} %get-tuple-element.20), channel_id=1, source_target_pairs={{480,0},{0,32},{32,64},{64,96},{96,128},{128,160},{160,192},{192,2... | collective-permute-start | bytes 737288 | tf_op jit(solution)/shard_map/ppermute | solution.py:17
  31.4 3.2 %collective-permute-start.3 = (bf16[960,128]{1,0:T(8,128)(2,1)S(1)}, bf16[960,128]{1,0:T(8,128)(2,1)S(1)}, u32[]{:S(2)}, u32[]{:S(2)}) collective-permute-start(bf16[960,128]{1,0:T(8,128)(2,1)S(1)} %get-tuple-element.21), channel_id=1, source_target_pairs={{448,0},{480,32},{0,64},{32,96},{64,128},{96,160},{128,192},{160,2... | collective-permute-start | bytes 737288 | tf_op jit(solution)/shard_map/ppermute | solution.py:17
  34.7 0.0 collective-permute-start.4
  34.7 3.3 %collective-permute-start.5 = (bf16[3,128,384]{2,1,0:T(8,128)(2,1)S(1)}, bf16[3,128,384]{2,1,0:T(8,128)(2,1)S(1)}, u32[]{:S(2)}, u32[]{:S(2)}) collective-permute-start(bf16[3,128,384]{2,1,0:T(8,128)(2,1)S(1)} %pad_maximum_fusion.here), channel_id=1, source_target_pairs={{64,0},{96,32},{128,64},{160,96},{192,128},{224,160},{256,192},{28... | collective-permute-start | bytes 884744 | tf_op jit(solution)/shard_map/ppermute | solution.py:17
  38.7 3.1 %collective-permute-done.3.second = bf16[960,128]{1,0:T(8,128)(2,1)S(1)} collective-permute-done((bf16[960,128]{1,0:T(8,128)(2,1)S(1)}, bf16[960,128]{1,0:T(8,128)(2,1)S(1)}, u32[]{:S(2)}, u32[]{:S(2)}) %collective-permute-start.3) | collective-permute-done | bytes 245792 | tf_op jit(solution)/shard_map/ppermute | solution.py:17
  41.8 1.5 %mid.1 = bf16[16,64,128]{2,1,0:T(8,128)(2,1)} custom-call(bf16[4,576,128]{2,1,0:T(8,128)(2,1)S(1)} %all-to-all-done.1.gathered, bf16[1,1,3,29,64,64]{5,4,3,2,1,0:T(8,128)(2,1)S(1)} %copy-done, bf16[960,128]{1,0:T(8,128)(2,1)S(1)} %collective-permute-done.2.first, bf16[960,128]{1,0:T(8,128)(2,1)S(1)} %collective-permute-done.3.second), custom_call_target="tpu_custom_call" | custom-call | flops 536870912 | bytes 3000000 | tf_op jit(solution)/shard_map/mid/pallas_call | solution.py:208
  43.2 7.6 %all-to-all-start.2 = ((bf16[16,64,128]{2,1,0:T(8,128)(2,1)}), bf16[16,64,128]{2,1,0:T(8,128)(2,1)S(1)}, u32[]{:S(2)}, u32[]{:S(2)}) async-start(bf16[16,64,128]{2,1,0:T(8,128)(2,1)} %mid.1), calls=%async_computation.2 | async-start | bytes 524288 | tf_op jit(solution)/shard_map/all_to_all | solution.py:216
  50.8 0.0 copy-start.2
  50.9 0.0 copy-start.3
  50.9 1.7 %copy-done.3 = bf16[1,1,9,384,384]{4,3,2,1,0:T(8,128)(2,1)S(1)} copy-done((bf16[1,1,9,384,384]{4,3,2,1,0:T(8,128)(2,1)S(1)}, bf16[1,1,9,384,384]{4,3,2,1,0:T(8,128)(2,1)}, u32[]{:S(2)}) %copy-start.3) | copy-done | bytes 2654232
  52.7 0.9 %copy-done.4 = bf16[1,16,64,64]{3,2,1,0:T(8,128)(2,1)S(1)} copy-done((bf16[1,16,64,64]{3,2,1,0:T(8,128)(2,1)S(1)}, bf16[1,16,64,64]{3,2,1,0:T(8,128)(2,1)}, u32[]{:S(2)}) %copy-start.4) | copy-done | bytes 131096
  53.6 2.0 %near.1 = (f32[128,384]{1,0:T(8,128)S(1)}, bf16[16,64,64]{2,1,0:T(8,128)(2,1)S(1)}) custom-call(s32[1,1,9]{2,1,0:T(1,128)S(1)} %copy-done.5, s32[1,1]{1,0:T(1,128)S(6)} %copy.12.count, s32[1,16]{1,0:T(1,128)S(1)} %copy-done.6, bf16[1,1,9,384,384]{4,3,2,1,0:T(8,128)(2,1)S(1)} %copy-done.3, bf16[3,128,384]{2,1,0:T(8,128)(2,1)S(1)} %pad_maximum_fusion.here, ...), custom_call_target="tpu_custom_call" | custom-call | flops 68719476736 | bytes 3538944 | tf_op jit(solution)/shard_map/near/pallas_call | solution.py:218
  55.6 6.9 %all-to-all-done.2.received = bf16[16,64,128]{2,1,0:T(8,128)(2,1)S(1)} async-done(((bf16[16,64,128]{2,1,0:T(8,128)(2,1)}), bf16[16,64,128]{2,1,0:T(8,128)(2,1)S(1)}, u32[]{:S(2)}, u32[]{:S(2)}) %all-to-all-start.2) | async-done | bytes 262176 | tf_op jit(solution)/shard_map/all_to_all | solution.py:216
  62.6 1.3 %final.1 = bf16[1,1,128,384]{3,2,1,0:T(8,128)(2,1)} custom-call(bf16[16,64,128]{2,1,0:T(8,128)(2,1)S(1)} %all-to-all-done.2.received, bf16[16,64,64]{2,1,0:T(8,128)(2,1)S(1)} %get-tuple-element.23.ordered, bf16[1,1,64,64]{3,2,1,0:T(8,128)(2,1)S(1)} %copy-done.2, bf16[1,1,64,384]{3,2,1,0:T(8,128)(2,1)S(1)} %copy-done.1, f32[128,384]{1,0:T(8,128)S(1)} %get-tuple-element.24.near), custom_call_target="tpu_custom_call" | custom-call | flops 29360128 | bytes 1000000 | tf_op jit(solution)/shard_map/final/pallas_call | solution.py:227
  (17 shorter events, 0.1 us)
Async XLA Ops:
  0.0 34.6 %copy-start.7 = (bf16[1,1,128,384]{3,2,1,0:T(8,128)(2,1)S(1)}, bf16[1,1,128,384]{3,2,1,0:T(8,128)(2,1)}, u32[]{:S(2)}) copy-start(bf16[1,1,128,384]{3,2,1,0:T(8,128)(2,1)} %vectors.1) | copy-start | bytes 294916
  0.0 28.1 %copy-start = (bf16[1,1,3,29,64,64]{5,4,3,2,1,0:T(8,128)(2,1)S(1)}, bf16[1,1,3,29,64,64]{5,4,3,2,1,0:T(8,128)(2,1)}, u32[]{:S(2)}) copy-start(bf16[1,1,3,29,64,64]{5,4,3,2,1,0:T(8,128)(2,1)} %own) | copy-start | bytes 2138116
  1.9 21.6 %all-to-all-start = ((bf16[8,96,128]{2,1,0:T(8,128)(2,1)}), bf16[8,96,128]{2,1,0:T(8,128)(2,1)S(1)}, u32[]{:S(2)}, u32[]{:S(2)}) async-start(bf16[8,96,128]{2,1,0:T(8,128)(2,1)} %leaf.1), calls=%async_computation | async-start | bytes 393216 | tf_op jit(solution)/shard_map/all_to_all | solution.py:178
  12.7 15.7 %collective-permute-start = (bf16[128,384]{1,0:T(8,128)(2,1)}, bf16[128,384]{1,0:T(8,128)(2,1)S(1)}, u32[]{:S(2)}, u32[]{:S(2)}) collective-permute-start(bf16[128,384]{1,0:T(8,128)(2,1)} %bitcast.4), channel_id=1, source_target_pairs={{1,0},{2,1},{3,2},{4,3},{5,4},{6,5},{7,6},{8,7},{9,8},{10,9},{11,1... | collective-permute-start | bytes 294920 | tf_op jit(solution)/shard_map/ppermute | solution.py:17
  19.5 8.9 %collective-permute-start.1 = (bf16[128,384]{1,0:T(8,128)(2,1)}, bf16[128,384]{1,0:T(8,128)(2,1)S(1)}, u32[]{:S(2)}, u32[]{:S(2)}) collective-permute-start(bf16[128,384]{1,0:T(8,128)(2,1)} %bitcast.5), channel_id=1, source_target_pairs={{2,0},{3,1},{4,2},{5,3},{6,4},{7,5},{8,6},{9,7},{10,8},{11,9},{12,... | collective-permute-start | bytes 294920 | tf_op jit(solution)/shard_map/ppermute | solution.py:17
  24.6 17.2 %all-to-all-start.1 = ((bf16[4,576,128]{2,1,0:T(8,128)(2,1)}), bf16[4,576,128]{2,1,0:T(8,128)(2,1)S(1)}, u32[]{:S(2)}, u32[]{:S(2)}) async-start(bf16[4,576,128]{2,1,0:T(8,128)(2,1)} %fold.1), calls=%async_computation.1 | async-start | bytes 1179648 | tf_op jit(solution)/shard_map/all_to_all | solution.py:188
  28.1 22.8 %copy-start.5 = (s32[1,1,9]{2,1,0:T(1,128)S(1)}, s32[1,1,9]{2,1,0:T(1,128)}, u32[]{:S(2)}) copy-start(s32[1,1,9]{2,1,0:T(1,128)} %source.1) | copy-start | bytes 112
  28.1 22.8 %copy-start.6 = (s32[1,16]{1,0:T(1,128)S(1)}, s32[1,16]{1,0:T(1,128)}, u32[]{:S(2)}) copy-start(s32[1,16]{1,0:T(1,128)} %listing.1) | copy-start | bytes 196
  28.4 10.2 %collective-permute-start.2 = (bf16[960,128]{1,0:T(8,128)(2,1)S(1)}, bf16[960,128]{1,0:T(8,128)(2,1)S(1)}, u32[]{:S(2)}, u32[]{:S(2)}) collective-permute-start(bf16[960,128]{1,0:T(8,128)(2,1)S(1)} %get-tuple-element.20), channel_id=1, source_target_pairs={{480,0},{0,32},{32,64},{64,96},{96,128},{128,160},{160,192},{192,2... | collective-permute-start | bytes 737288 | tf_op jit(solution)/shard_map/ppermute | solution.py:17
  31.4 10.3 %collective-permute-start.3 = (bf16[960,128]{1,0:T(8,128)(2,1)S(1)}, bf16[960,128]{1,0:T(8,128)(2,1)S(1)}, u32[]{:S(2)}, u32[]{:S(2)}) collective-permute-start(bf16[960,128]{1,0:T(8,128)(2,1)S(1)} %get-tuple-element.21), channel_id=1, source_target_pairs={{448,0},{480,32},{0,64},{32,96},{64,128},{96,160},{128,192},{160,2... | collective-permute-start | bytes 737288 | tf_op jit(solution)/shard_map/ppermute | solution.py:17
  34.7 16.2 %collective-permute-start.4 = (bf16[3,128,384]{2,1,0:T(8,128)(2,1)S(1)}, bf16[3,128,384]{2,1,0:T(8,128)(2,1)S(1)}, u32[]{:S(2)}, u32[]{:S(2)}) collective-permute-start(bf16[3,128,384]{2,1,0:T(8,128)(2,1)S(1)} %pad_maximum_fusion.here), channel_id=1, source_target_pairs={{32,0},{64,32},{96,64},{128,96},{160,128},{192,160},{224,192},{256... | collective-permute-start | bytes 884744 | tf_op jit(solution)/shard_map/ppermute | solution.py:17
  34.7 16.1 %collective-permute-start.5 = (bf16[3,128,384]{2,1,0:T(8,128)(2,1)S(1)}, bf16[3,128,384]{2,1,0:T(8,128)(2,1)S(1)}, u32[]{:S(2)}, u32[]{:S(2)}) collective-permute-start(bf16[3,128,384]{2,1,0:T(8,128)(2,1)S(1)} %pad_maximum_fusion.here), channel_id=1, source_target_pairs={{64,0},{96,32},{128,64},{160,96},{192,128},{224,160},{256,192},{28... | collective-permute-start | bytes 884744 | tf_op jit(solution)/shard_map/ppermute | solution.py:17
  43.2 19.3 %all-to-all-start.2 = ((bf16[16,64,128]{2,1,0:T(8,128)(2,1)}), bf16[16,64,128]{2,1,0:T(8,128)(2,1)S(1)}, u32[]{:S(2)}, u32[]{:S(2)}) async-start(bf16[16,64,128]{2,1,0:T(8,128)(2,1)} %mid.1), calls=%async_computation.2 | async-start | bytes 524288 | tf_op jit(solution)/shard_map/all_to_all | solution.py:216
  50.8 11.7 %copy-start.1 = (bf16[1,1,64,384]{3,2,1,0:T(8,128)(2,1)S(1)}, bf16[1,1,64,384]{3,2,1,0:T(8,128)(2,1)}, u32[]{:S(2)}) copy-start(bf16[1,1,64,384]{3,2,1,0:T(8,128)(2,1)} %basis.3) | copy-start | bytes 147460
  50.8 11.7 %copy-start.2 = (bf16[1,1,64,64]{3,2,1,0:T(8,128)(2,1)S(1)}, bf16[1,1,64,64]{3,2,1,0:T(8,128)(2,1)}, u32[]{:S(2)}) copy-start(bf16[1,1,64,64]{3,2,1,0:T(8,128)(2,1)} %transfer.3) | copy-start | bytes 24580
  50.9 1.8 %copy-start.3 = (bf16[1,1,9,384,384]{4,3,2,1,0:T(8,128)(2,1)S(1)}, bf16[1,1,9,384,384]{4,3,2,1,0:T(8,128)(2,1)}, u32[]{:S(2)}) copy-start(bf16[1,1,9,384,384]{4,3,2,1,0:T(8,128)(2,1)} %blocks.1) | copy-start | bytes 7962628
  52.7 0.9 %copy-start.4 = (bf16[1,16,64,64]{3,2,1,0:T(8,128)(2,1)S(1)}, bf16[1,16,64,64]{3,2,1,0:T(8,128)(2,1)}, u32[]{:S(2)}) copy-start(bf16[1,16,64,64]{3,2,1,0:T(8,128)(2,1)} %coupling.1) | copy-start | bytes 393220

commit v4 on v3

--- a/solution.py
+++ b/solution.py
@@ -38,18 +38,34 @@
         out[i] = chunk
 
 
-def fold_kernel(gathered, out):
+def fold_kernel(gathered, out, chunk, sems):
     lines, depth = gathered.shape[0], gathered.shape[1]
     rank = 2 * depth // 3
     half = rank // 2
+    size = lines * rank
+
+    def send(part, start, length):
+        return [
+            pltpu.make_async_copy(
+                chunk.at[pl.ds(start, length)], out.at[i, pl.ds(start, length)], sems.at[part, i]
+            )
+            for i in range(out.shape[0])
+        ]
+
+    chunk[:size] = gathered[:, :rank].reshape(size, -1)
+    leaves = send(0, 0, size)
+    for copy in leaves:
+        copy.start()
     low = gathered[:, :half].reshape(lines * half, -1)
     high = gathered[:, half:rank].reshape(lines * half, -1)
     packed = gathered[:, rank:].reshape(lines * half, -1)
     region = contract_rows(packed[:, :rank], low) + contract_rows(packed[:, rank:], high)
-    leaves = gathered[:, :rank].reshape(lines * rank, -1)
-    chunk = jnp.concatenate([leaves, region.astype(out.dtype)], axis=0)
-    for i in range(out.shape[0]):
-        out[i] = chunk
+    chunk[size:] = region.astype(chunk.dtype)
+    regions = send(1, size, rank)
+    for copy in regions:
+        copy.start()
+    for copy in leaves + regions:
+        copy.wait()
 
 
 def pack_kernel(couple, out_first, out_second):
@@ -126,12 +142,12 @@
     return pl.BlockSpec(shape, lambda i: (0,) * len(shape))
 
 
-def call(kernel, out_shape, in_specs, scratch, cost, name):
+def call(kernel, out_shape, in_specs, scratch, cost, name, out_space=VMEM):
     return pl.pallas_call(
         kernel,
         out_shape=out_shape,
         in_specs=in_specs,
-        out_specs=jax.tree.map(lambda _: pl.BlockSpec(memory_space=VMEM), out_shape),
+        out_specs=jax.tree.map(lambda _: pl.BlockSpec(memory_space=out_space), out_shape),
         scratch_shapes=scratch,
         cost_estimate=pl.CostEstimate(flops=cost[0], bytes_accessed=cost[1], transcendentals=0),
         compiler_params=pltpu.CompilerParams(vmem_limit_bytes=VL * 1024 * 1024),
@@ -181,9 +197,10 @@
         fold_kernel,
         jax.ShapeDtypeStruct(folded_shape, bf16),
         [vmem],
-        [],
+        [VMEM(folded_shape[1:], bf16), pltpu.SemaphoreType.DMA((2, groups))],
         (2 * LINES * rank * rank * vecs, 1000000),
         "fold",
+        pl.ANY,
     )(line)
     gathered = lax.all_to_all(folded, "col", 0, 0, axis_index_groups=far_cols, tiled=True)
 

time: 64.3 us -> 64.2 us (level)
  Pallas kernels: 7.96 us -> 7.21 us
  waiting for transfers between devices: 10 us -> 10.7 us
  transfers between devices with their start and end apart: 9 -> 9, of which waited for: 2 -> 2; matrix products, arithmetic and copies ran while one was open for 0% -> 0% of each run, Pallas kernels for 8% -> 6%
where the time goes in v4:
time: 64.2 us; the launch traced here: 63.7 us
  starting transfers between devices  42.2 us (66%)
  waiting for transfers between devices  10.7 us (17%)
  Pallas kernels  7.21 us (11%)
  local copies, waits for them, and re-layouts  2.72 us (4%)
  between operations  0.84 us (1%)
    ppermute x6, starting transfers between devices, shifted(): lax.ppermute(value, axis, [((i + steps) % count, i) for i in range(count)])  20.2 us
    all_to_all x1, starting transfers between devices, per_device(): lax.all_to_all(chunks, 'col', 0, 0, axis_index_groups=near_cols, tiled=True)  10.9 us
    all_to_all x1, starting transfers between devices, per_device(): lax.all_to_all(outgoing, 'row', split_axis=0, concat_axis=0, tiled=True)  7.62 us
    all_to_all x1, waiting for transfers between devices, per_device(): lax.all_to_all(outgoing, 'row', split_axis=0, concat_axis=0, tiled=True)  7.58 us
    all_to_all x1, starting transfers between devices, per_device(): lax.all_to_all(folded, 'col', 0, 0, axis_index_groups=far_cols, tiled=True)  3.49 us
    ppermute x6, waiting for transfers between devices, shifted(): lax.ppermute(value, axis, [((i + steps) % count, i) for i in range(count)])  3.09 us
    unnamed x16, local copies, waits for them, and re-layouts  2.72 us
    pallas_call x1, Pallas kernels, per_device(): pl.pallas_call(leaf_kernel, grid=(1,), out_shape=jax.ShapeDtypeStruct(chu...  1.87 us
  transfers between devices with their start and end apart: 9, of which 2 were waited for; matrix products, arithmetic and copies ran while one was open for 0% of the time, Pallas kernels for 6%

profile of v4, /device:TPU:1, one launch (start us, length us, event | category | flops | bytes accessed | tf_op | source)
XLA Modules:
  0.0 63.7 jit_solution(4711844709678631893)
XLA Ops:
  0.0 1.9 %leaf.1 = bf16[8,96,128]{2,1,0:T(8,128)(2,1)} custom-call(bf16[1,1,128,384]{3,2,1,0:T(8,128)(2,1)} %vectors.1, bf16[1,1,64,384]{3,2,1,0:T(8,128)(2,1)} %basis.2, bf16[1,1,64,64]{3,2,1,0:T(8,128)(2,1)} %transfer.2), custom_call_target="tpu_custom_call" | custom-call | flops 6291456 | bytes 1000000 | tf_op jit(solution)/shard_map/leaf/pallas_call | solution.py:183
  1.9 10.9 %all-to-all-start = ((bf16[8,96,128]{2,1,0:T(8,128)(2,1)}), bf16[8,96,128]{2,1,0:T(8,128)(2,1)S(1)}, u32[]{:S(2)}, u32[]{:S(2)}) async-start(bf16[8,96,128]{2,1,0:T(8,128)(2,1)} %leaf.1), calls=%async_computation | async-start | bytes 393216 | tf_op jit(solution)/shard_map/all_to_all | solution.py:194
  12.7 6.8 %collective-permute-start = (bf16[128,384]{1,0:T(8,128)(2,1)}, bf16[128,384]{1,0:T(8,128)(2,1)S(1)}, u32[]{:S(2)}, u32[]{:S(2)}) collective-permute-start(bf16[128,384]{1,0:T(8,128)(2,1)} %bitcast.4), channel_id=1, source_target_pairs={{1,0},{2,1},{3,2},{4,3},{5,4},{6,5},{7,6},{8,7},{9,8},{10,9},{11,1... | collective-permute-start | bytes 294920 | tf_op jit(solution)/shard_map/ppermute | solution.py:17
  19.5 4.0 %collective-permute-start.1 = (bf16[128,384]{1,0:T(8,128)(2,1)}, bf16[128,384]{1,0:T(8,128)(2,1)S(1)}, u32[]{:S(2)}, u32[]{:S(2)}) collective-permute-start(bf16[128,384]{1,0:T(8,128)(2,1)} %bitcast.5), channel_id=1, source_target_pairs={{2,0},{3,1},{4,2},{5,3},{6,4},{7,5},{8,6},{9,7},{10,8},{11,9},{12,... | collective-permute-start | bytes 294920 | tf_op jit(solution)/shard_map/ppermute | solution.py:17
  23.5 1.0 %fold.1 = bf16[4,576,128]{2,1,0:T(8,128)(2,1)} custom-call(bf16[8,96,128]{2,1,0:T(8,128)(2,1)S(1)} %all-to-all-done.gathered), custom_call_target="tpu_custom_call" | custom-call | flops 8388608 | bytes 1000000 | tf_op jit(solution)/shard_map/fold/pallas_call | solution.py:196
  24.5 3.5 %all-to-all-start.1 = ((bf16[4,576,128]{2,1,0:T(8,128)(2,1)}), bf16[4,576,128]{2,1,0:T(8,128)(2,1)S(1)}, u32[]{:S(2)}, u32[]{:S(2)}) async-start(bf16[4,576,128]{2,1,0:T(8,128)(2,1)} %fold.1), calls=%async_computation.1 | async-start | bytes 1179648 | tf_op jit(solution)/shard_map/all_to_all | solution.py:205
  28.0 0.0 copy-start.5
  28.0 0.0 copy-start.6
  28.0 0.3 pack.1
  28.3 0.0 collective-permute-done
  28.3 3.0 %collective-permute-start.2 = (bf16[960,128]{1,0:T(8,128)(2,1)S(1)}, bf16[960,128]{1,0:T(8,128)(2,1)S(1)}, u32[]{:S(2)}, u32[]{:S(2)}) collective-permute-start(bf16[960,128]{1,0:T(8,128)(2,1)S(1)} %get-tuple-element.20), channel_id=1, source_target_pairs={{480,0},{0,32},{32,64},{64,96},{96,128},{128,160},{160,192},{192,2... | collective-permute-start | bytes 737288 | tf_op jit(solution)/shard_map/ppermute | solution.py:17
  31.3 3.2 %collective-permute-start.3 = (bf16[960,128]{1,0:T(8,128)(2,1)S(1)}, bf16[960,128]{1,0:T(8,128)(2,1)S(1)}, u32[]{:S(2)}, u32[]{:S(2)}) collective-permute-start(bf16[960,128]{1,0:T(8,128)(2,1)S(1)} %get-tuple-element.21), channel_id=1, source_target_pairs={{448,0},{480,32},{0,64},{32,96},{64,128},{96,160},{128,192},{160,2... | collective-permute-start | bytes 737288 | tf_op jit(solution)/shard_map/ppermute | solution.py:17
  34.6 0.0 collective-permute-start.4
  34.6 3.3 %collective-permute-start.5 = (bf16[3,128,384]{2,1,0:T(8,128)(2,1)S(1)}, bf16[3,128,384]{2,1,0:T(8,128)(2,1)S(1)}, u32[]{:S(2)}, u32[]{:S(2)}) collective-permute-start(bf16[3,128,384]{2,1,0:T(8,128)(2,1)S(1)} %pad_maximum_fusion.here), channel_id=1, source_target_pairs={{64,0},{96,32},{128,64},{160,96},{192,128},{224,160},{256,192},{28... | collective-permute-start | bytes 884744 | tf_op jit(solution)/shard_map/ppermute | solution.py:17
  38.6 3.1 %collective-permute-done.3.second = bf16[960,128]{1,0:T(8,128)(2,1)S(1)} collective-permute-done((bf16[960,128]{1,0:T(8,128)(2,1)S(1)}, bf16[960,128]{1,0:T(8,128)(2,1)S(1)}, u32[]{:S(2)}, u32[]{:S(2)}) %collective-permute-start.3) | collective-permute-done | bytes 245792 | tf_op jit(solution)/shard_map/ppermute | solution.py:17
  41.7 1.5 %mid.1 = bf16[16,64,128]{2,1,0:T(8,128)(2,1)} custom-call(bf16[4,576,128]{2,1,0:T(8,128)(2,1)S(1)} %all-to-all-done.1.gathered, bf16[1,1,3,29,64,64]{5,4,3,2,1,0:T(8,128)(2,1)S(1)} %copy-done, bf16[960,128]{1,0:T(8,128)(2,1)S(1)} %collective-permute-done.2.first, bf16[960,128]{1,0:T(8,128)(2,1)S(1)} %collective-permute-done.3.second), custom_call_target="tpu_custom_call" | custom-call | flops 536870912 | bytes 3000000 | tf_op jit(solution)/shard_map/mid/pallas_call | solution.py:225
  43.1 7.6 %all-to-all-start.2 = ((bf16[16,64,128]{2,1,0:T(8,128)(2,1)}), bf16[16,64,128]{2,1,0:T(8,128)(2,1)S(1)}, u32[]{:S(2)}, u32[]{:S(2)}) async-start(bf16[16,64,128]{2,1,0:T(8,128)(2,1)} %mid.1), calls=%async_computation.2 | async-start | bytes 524288 | tf_op jit(solution)/shard_map/all_to_all | solution.py:233
  50.7 0.0 copy-start.2
  50.8 0.0 copy-start.3
  50.8 1.7 %copy-done.3 = bf16[1,1,9,384,384]{4,3,2,1,0:T(8,128)(2,1)S(1)} copy-done((bf16[1,1,9,384,384]{4,3,2,1,0:T(8,128)(2,1)S(1)}, bf16[1,1,9,384,384]{4,3,2,1,0:T(8,128)(2,1)}, u32[]{:S(2)}) %copy-start.3) | copy-done | bytes 2654232
  52.6 0.9 %copy-done.4 = bf16[1,16,64,64]{3,2,1,0:T(8,128)(2,1)S(1)} copy-done((bf16[1,16,64,64]{3,2,1,0:T(8,128)(2,1)S(1)}, bf16[1,16,64,64]{3,2,1,0:T(8,128)(2,1)}, u32[]{:S(2)}) %copy-start.4) | copy-done | bytes 131096
  53.5 1.4 %near.1 = (f32[128,384]{1,0:T(8,128)S(1)}, bf16[16,64,64]{2,1,0:T(8,128)(2,1)S(1)}) custom-call(s32[1,1,9]{2,1,0:T(1,128)S(1)} %copy-done.5, s32[1,1]{1,0:T(1,128)S(6)} %copy.12.count, s32[1,16]{1,0:T(1,128)S(1)} %copy-done.6, bf16[1,1,9,384,384]{4,3,2,1,0:T(8,128)(2,1)S(1)} %copy-done.3, bf16[3,128,384]{2,1,0:T(8,128)(2,1)S(1)} %pad_maximum_fusion.here, ...), custom_call_target="tpu_custom_call" | custom-call | flops 68719476736 | bytes 3538944 | tf_op jit(solution)/shard_map/near/pallas_call | solution.py:235
  54.9 7.6 %all-to-all-done.2.received = bf16[16,64,128]{2,1,0:T(8,128)(2,1)S(1)} async-done(((bf16[16,64,128]{2,1,0:T(8,128)(2,1)}), bf16[16,64,128]{2,1,0:T(8,128)(2,1)S(1)}, u32[]{:S(2)}, u32[]{:S(2)}) %all-to-all-start.2) | async-done | bytes 262176 | tf_op jit(solution)/shard_map/all_to_all | solution.py:233
  62.5 1.3 %final.1 = bf16[1,1,128,384]{3,2,1,0:T(8,128)(2,1)} custom-call(bf16[16,64,128]{2,1,0:T(8,128)(2,1)S(1)} %all-to-all-done.2.received, bf16[16,64,64]{2,1,0:T(8,128)(2,1)S(1)} %get-tuple-element.23.ordered, bf16[1,1,64,64]{3,2,1,0:T(8,128)(2,1)S(1)} %copy-done.2, bf16[1,1,64,384]{3,2,1,0:T(8,128)(2,1)S(1)} %copy-done.1, f32[128,384]{1,0:T(8,128)S(1)} %get-tuple-element.24.near), custom_call_target="tpu_custom_call" | custom-call | flops 29360128 | bytes 1000000 | tf_op jit(solution)/shard_map/final/pallas_call | solution.py:244
  (17 shorter events, 0.1 us)
Async XLA Ops:
  0.0 34.5 %copy-start.7 = (bf16[1,1,128,384]{3,2,1,0:T(8,128)(2,1)S(1)}, bf16[1,1,128,384]{3,2,1,0:T(8,128)(2,1)}, u32[]{:S(2)}) copy-start(bf16[1,1,128,384]{3,2,1,0:T(8,128)(2,1)} %vectors.1) | copy-start | bytes 294916
  0.0 28.0 %copy-start = (bf16[1,1,3,29,64,64]{5,4,3,2,1,0:T(8,128)(2,1)S(1)}, bf16[1,1,3,29,64,64]{5,4,3,2,1,0:T(8,128)(2,1)}, u32[]{:S(2)}) copy-start(bf16[1,1,3,29,64,64]{5,4,3,2,1,0:T(8,128)(2,1)} %own) | copy-start | bytes 2138116
  1.9 21.6 %all-to-all-start = ((bf16[8,96,128]{2,1,0:T(8,128)(2,1)}), bf16[8,96,128]{2,1,0:T(8,128)(2,1)S(1)}, u32[]{:S(2)}, u32[]{:S(2)}) async-start(bf16[8,96,128]{2,1,0:T(8,128)(2,1)} %leaf.1), calls=%async_computation | async-start | bytes 393216 | tf_op jit(solution)/shard_map/all_to_all | solution.py:194
  12.7 15.6 %collective-permute-start = (bf16[128,384]{1,0:T(8,128)(2,1)}, bf16[128,384]{1,0:T(8,128)(2,1)S(1)}, u32[]{:S(2)}, u32[]{:S(2)}) collective-permute-start(bf16[128,384]{1,0:T(8,128)(2,1)} %bitcast.4), channel_id=1, source_target_pairs={{1,0},{2,1},{3,2},{4,3},{5,4},{6,5},{7,6},{8,7},{9,8},{10,9},{11,1... | collective-permute-start | bytes 294920 | tf_op jit(solution)/shard_map/ppermute | solution.py:17
  19.5 8.8 %collective-permute-start.1 = (bf16[128,384]{1,0:T(8,128)(2,1)}, bf16[128,384]{1,0:T(8,128)(2,1)S(1)}, u32[]{:S(2)}, u32[]{:S(2)}) collective-permute-start(bf16[128,384]{1,0:T(8,128)(2,1)} %bitcast.5), channel_id=1, source_target_pairs={{2,0},{3,1},{4,2},{5,3},{6,4},{7,5},{8,6},{9,7},{10,8},{11,9},{12,... | collective-permute-start | bytes 294920 | tf_op jit(solution)/shard_map/ppermute | solution.py:17
  24.5 17.2 %all-to-all-start.1 = ((bf16[4,576,128]{2,1,0:T(8,128)(2,1)}), bf16[4,576,128]{2,1,0:T(8,128)(2,1)S(1)}, u32[]{:S(2)}, u32[]{:S(2)}) async-start(bf16[4,576,128]{2,1,0:T(8,128)(2,1)} %fold.1), calls=%async_computation.1 | async-start | bytes 1179648 | tf_op jit(solution)/shard_map/all_to_all | solution.py:205
  28.0 22.8 %copy-start.5 = (s32[1,1,9]{2,1,0:T(1,128)S(1)}, s32[1,1,9]{2,1,0:T(1,128)}, u32[]{:S(2)}) copy-start(s32[1,1,9]{2,1,0:T(1,128)} %source.1) | copy-start | bytes 112
  28.0 22.8 %copy-start.6 = (s32[1,16]{1,0:T(1,128)S(1)}, s32[1,16]{1,0:T(1,128)}, u32[]{:S(2)}) copy-start(s32[1,16]{1,0:T(1,128)} %listing.1) | copy-start | bytes 196
  28.3 10.2 %collective-permute-start.2 = (bf16[960,128]{1,0:T(8,128)(2,1)S(1)}, bf16[960,128]{1,0:T(8,128)(2,1)S(1)}, u32[]{:S(2)}, u32[]{:S(2)}) collective-permute-start(bf16[960,128]{1,0:T(8,128)(2,1)S(1)} %get-tuple-element.20), channel_id=1, source_target_pairs={{480,0},{0,32},{32,64},{64,96},{96,128},{128,160},{160,192},{192,2... | collective-permute-start | bytes 737288 | tf_op jit(solution)/shard_map/ppermute | solution.py:17
  31.3 10.3 %collective-permute-start.3 = (bf16[960,128]{1,0:T(8,128)(2,1)S(1)}, bf16[960,128]{1,0:T(8,128)(2,1)S(1)}, u32[]{:S(2)}, u32[]{:S(2)}) collective-permute-start(bf16[960,128]{1,0:T(8,128)(2,1)S(1)} %get-tuple-element.21), channel_id=1, source_target_pairs={{448,0},{480,32},{0,64},{32,96},{64,128},{96,160},{128,192},{160,2... | collective-permute-start | bytes 737288 | tf_op jit(solution)/shard_map/ppermute | solution.py:17
  34.6 16.2 %collective-permute-start.4 = (bf16[3,128,384]{2,1,0:T(8,128)(2,1)S(1)}, bf16[3,128,384]{2,1,0:T(8,128)(2,1)S(1)}, u32[]{:S(2)}, u32[]{:S(2)}) collective-permute-start(bf16[3,128,384]{2,1,0:T(8,128)(2,1)S(1)} %pad_maximum_fusion.here), channel_id=1, source_target_pairs={{32,0},{64,32},{96,64},{128,96},{160,128},{192,160},{224,192},{256... | collective-permute-start | bytes 884744 | tf_op jit(solution)/shard_map/ppermute | solution.py:17
  34.6 16.1 %collective-permute-start.5 = (bf16[3,128,384]{2,1,0:T(8,128)(2,1)S(1)}, bf16[3,128,384]{2,1,0:T(8,128)(2,1)S(1)}, u32[]{:S(2)}, u32[]{:S(2)}) collective-permute-start(bf16[3,128,384]{2,1,0:T(8,128)(2,1)S(1)} %pad_maximum_fusion.here), channel_id=1, source_target_pairs={{64,0},{96,32},{128,64},{160,96},{192,128},{224,160},{256,192},{28... | collective-permute-start | bytes 884744 | tf_op jit(solution)/shard_map/ppermute | solution.py:17
  43.1 19.3 %all-to-all-start.2 = ((bf16[16,64,128]{2,1,0:T(8,128)(2,1)}), bf16[16,64,128]{2,1,0:T(8,128)(2,1)S(1)}, u32[]{:S(2)}, u32[]{:S(2)}) async-start(bf16[16,64,128]{2,1,0:T(8,128)(2,1)} %mid.1), calls=%async_computation.2 | async-start | bytes 524288 | tf_op jit(solution)/shard_map/all_to_all | solution.py:233
  50.7 11.7 %copy-start.1 = (bf16[1,1,64,384]{3,2,1,0:T(8,128)(2,1)S(1)}, bf16[1,1,64,384]{3,2,1,0:T(8,128)(2,1)}, u32[]{:S(2)}) copy-start(bf16[1,1,64,384]{3,2,1,0:T(8,128)(2,1)} %basis.3) | copy-start | bytes 147460
  50.7 11.7 %copy-start.2 = (bf16[1,1,64,64]{3,2,1,0:T(8,128)(2,1)S(1)}, bf16[1,1,64,64]{3,2,1,0:T(8,128)(2,1)}, u32[]{:S(2)}) copy-start(bf16[1,1,64,64]{3,2,1,0:T(8,128)(2,1)} %transfer.3) | copy-start | bytes 24580
  50.8 1.8 %copy-start.3 = (bf16[1,1,9,384,384]{4,3,2,1,0:T(8,128)(2,1)S(1)}, bf16[1,1,9,384,384]{4,3,2,1,0:T(8,128)(2,1)}, u32[]{:S(2)}) copy-start(bf16[1,1,9,384,384]{4,3,2,1,0:T(8,128)(2,1)} %blocks.1) | copy-start | bytes 7962628
  52.6 0.9 %copy-start.4 = (bf16[1,16,64,64]{3,2,1,0:T(8,128)(2,1)S(1)}, bf16[1,16,64,64]{3,2,1,0:T(8,128)(2,1)}, u32[]{:S(2)}) copy-start(bf16[1,16,64,64]{3,2,1,0:T(8,128)(2,1)} %coupling.1) | copy-start | bytes 393220

commit v5 on v4

--- a/solution.py
+++ b/solution.py
@@ -21,10 +21,10 @@
     return lax.dot_general(left, right, (((0,), (0,)), ((), ())), preferred_element_type=jnp.float32)
 
 
-def exact_rows(left, right):
-    high = right.astype(jnp.bfloat16)
-    low = (right - high.astype(jnp.float32)).astype(jnp.bfloat16)
-    return contract_rows(left, high) + contract_rows(left, low)
+def two_parts(exact, value):
+    high = value.astype(jnp.bfloat16)
+    low = (value - high.astype(jnp.float32)).astype(jnp.bfloat16)
+    return jnp.concatenate([high, low], axis=0), jnp.concatenate([exact, exact], axis=0)
 
 
 def leaf_kernel(vectors, basis, transfer, out):
@@ -131,10 +131,10 @@
     outgoing = contract_rows(
         ordered[...].reshape(rows * rank, rank), received[...].reshape(rows * rank, received.shape[2])
     )
-    leaf_out = band + exact_rows(transfer[0, 0], outgoing)
-    high = leaf_out.astype(jnp.bfloat16)
-    low = (leaf_out - high.astype(jnp.float32)).astype(jnp.bfloat16)
-    far = contract_rows(high, basis[0, 0]) + contract_rows(low, basis[0, 0])
+    parts, weights = two_parts(transfer[0, 0], outgoing)
+    leaf_out = band + contract_rows(weights, parts)
+    parts, weights = two_parts(basis[0, 0], leaf_out)
+    far = contract_rows(parts, weights)
     out[0, 0] = (near[...] + far).astype(out.dtype)
 
 

time: 64.2 us -> 64.2 us (level)
  waiting for transfers between devices: 10.7 us -> 9.83 us
  Pallas kernels: 7.21 us -> 8.01 us
    pallas_call x1, Pallas kernels: 1.36 us -> 2.2 us  [per_device(): call(near_kernel, [jax.ShapeDtypeStruct((vecs, leaf), f32), jax.ShapeDtyp...]
    all_to_all x1, waiting for transfers between devices: 7.58 us -> 6.74 us  [per_device(): lax.all_to_all(outgoing, 'row', split_axis=0, concat_axis=0, tiled=True)]
  transfers between devices with their start and end apart: 9 -> 9, of which waited for: 2 -> 2; matrix products, arithmetic and copies ran while one was open for 0% -> 0% of each run, Pallas kernels for 6% -> 8%
where the time goes in v5:
time: 64.2 us; the launch traced here: 63.7 us
  starting transfers between devices  42.2 us (66%)
  waiting for transfers between devices  9.83 us (15%)
  Pallas kernels  8.01 us (12%)
  local copies, waits for them, and re-layouts  2.72 us (4%)
  between operations  0.84 us (1%)
    ppermute x6, starting transfers between devices, shifted(): lax.ppermute(value, axis, [((i + steps) % count, i) for i in range(count)])  20.2 us
    all_to_all x1, starting transfers between devices, per_device(): lax.all_to_all(chunks, 'col', 0, 0, axis_index_groups=near_cols, tiled=True)  10.9 us
    all_to_all x1, starting transfers between devices, per_device(): lax.all_to_all(outgoing, 'row', split_axis=0, concat_axis=0, tiled=True)  7.62 us
    all_to_all x1, waiting for transfers between devices, per_device(): lax.all_to_all(outgoing, 'row', split_axis=0, concat_axis=0, tiled=True)  6.74 us
    all_to_all x1, starting transfers between devices, per_device(): lax.all_to_all(folded, 'col', 0, 0, axis_index_groups=far_cols, tiled=True)  3.49 us
    ppermute x6, waiting for transfers between devices, shifted(): lax.ppermute(value, axis, [((i + steps) % count, i) for i in range(count)])  3.09 us
    unnamed x16, local copies, waits for them, and re-layouts  2.72 us
    pallas_call x1, Pallas kernels, per_device(): call(near_kernel, [jax.ShapeDtypeStruct((vecs, leaf), f32), jax.ShapeDtyp...  2.2 us
  transfers between devices with their start and end apart: 9, of which 2 were waited for; matrix products, arithmetic and copies ran while one was open for 0% of the time, Pallas kernels for 8%

profile of v5, /device:TPU:1, one launch (start us, length us, event | category | flops | bytes accessed | tf_op | source)
XLA Modules:
  0.0 63.7 jit_solution(13162553297635424203)
XLA Ops:
  0.0 1.9 %leaf.1 = bf16[8,96,128]{2,1,0:T(8,128)(2,1)} custom-call(bf16[1,1,128,384]{3,2,1,0:T(8,128)(2,1)} %vectors.1, bf16[1,1,64,384]{3,2,1,0:T(8,128)(2,1)} %basis.2, bf16[1,1,64,64]{3,2,1,0:T(8,128)(2,1)} %transfer.2), custom_call_target="tpu_custom_call" | custom-call | flops 6291456 | bytes 1000000 | tf_op jit(solution)/shard_map/leaf/pallas_call | solution.py:183
  1.9 10.9 %all-to-all-start = ((bf16[8,96,128]{2,1,0:T(8,128)(2,1)}), bf16[8,96,128]{2,1,0:T(8,128)(2,1)S(1)}, u32[]{:S(2)}, u32[]{:S(2)}) async-start(bf16[8,96,128]{2,1,0:T(8,128)(2,1)} %leaf.1), calls=%async_computation | async-start | bytes 393216 | tf_op jit(solution)/shard_map/all_to_all | solution.py:194
  12.7 6.8 %collective-permute-start = (bf16[128,384]{1,0:T(8,128)(2,1)}, bf16[128,384]{1,0:T(8,128)(2,1)S(1)}, u32[]{:S(2)}, u32[]{:S(2)}) collective-permute-start(bf16[128,384]{1,0:T(8,128)(2,1)} %bitcast.4), channel_id=1, source_target_pairs={{1,0},{2,1},{3,2},{4,3},{5,4},{6,5},{7,6},{8,7},{9,8},{10,9},{11,1... | collective-permute-start | bytes 294920 | tf_op jit(solution)/shard_map/ppermute | solution.py:17
  19.5 4.0 %collective-permute-start.1 = (bf16[128,384]{1,0:T(8,128)(2,1)}, bf16[128,384]{1,0:T(8,128)(2,1)S(1)}, u32[]{:S(2)}, u32[]{:S(2)}) collective-permute-start(bf16[128,384]{1,0:T(8,128)(2,1)} %bitcast.5), channel_id=1, source_target_pairs={{2,0},{3,1},{4,2},{5,3},{6,4},{7,5},{8,6},{9,7},{10,8},{11,9},{12,... | collective-permute-start | bytes 294920 | tf_op jit(solution)/shard_map/ppermute | solution.py:17
  23.5 1.0 %fold.1 = bf16[4,576,128]{2,1,0:T(8,128)(2,1)} custom-call(bf16[8,96,128]{2,1,0:T(8,128)(2,1)S(1)} %all-to-all-done.gathered), custom_call_target="tpu_custom_call" | custom-call | flops 8388608 | bytes 1000000 | tf_op jit(solution)/shard_map/fold/pallas_call | solution.py:196
  24.5 3.5 %all-to-all-start.1 = ((bf16[4,576,128]{2,1,0:T(8,128)(2,1)}), bf16[4,576,128]{2,1,0:T(8,128)(2,1)S(1)}, u32[]{:S(2)}, u32[]{:S(2)}) async-start(bf16[4,576,128]{2,1,0:T(8,128)(2,1)} %fold.1), calls=%async_computation.1 | async-start | bytes 1179648 | tf_op jit(solution)/shard_map/all_to_all | solution.py:205
  28.0 0.0 copy-start.5
  28.0 0.0 copy-start.6
  28.0 0.3 pack.1
  28.3 0.0 collective-permute-done
  28.3 3.0 %collective-permute-start.2 = (bf16[960,128]{1,0:T(8,128)(2,1)S(1)}, bf16[960,128]{1,0:T(8,128)(2,1)S(1)}, u32[]{:S(2)}, u32[]{:S(2)}) collective-permute-start(bf16[960,128]{1,0:T(8,128)(2,1)S(1)} %get-tuple-element.20), channel_id=1, source_target_pairs={{480,0},{0,32},{32,64},{64,96},{96,128},{128,160},{160,192},{192,2... | collective-permute-start | bytes 737288 | tf_op jit(solution)/shard_map/ppermute | solution.py:17
  31.3 3.2 %collective-permute-start.3 = (bf16[960,128]{1,0:T(8,128)(2,1)S(1)}, bf16[960,128]{1,0:T(8,128)(2,1)S(1)}, u32[]{:S(2)}, u32[]{:S(2)}) collective-permute-start(bf16[960,128]{1,0:T(8,128)(2,1)S(1)} %get-tuple-element.21), channel_id=1, source_target_pairs={{448,0},{480,32},{0,64},{32,96},{64,128},{96,160},{128,192},{160,2... | collective-permute-start | bytes 737288 | tf_op jit(solution)/shard_map/ppermute | solution.py:17
  34.6 0.0 collective-permute-start.4
  34.6 3.3 %collective-permute-start.5 = (bf16[3,128,384]{2,1,0:T(8,128)(2,1)S(1)}, bf16[3,128,384]{2,1,0:T(8,128)(2,1)S(1)}, u32[]{:S(2)}, u32[]{:S(2)}) collective-permute-start(bf16[3,128,384]{2,1,0:T(8,128)(2,1)S(1)} %pad_maximum_fusion.here), channel_id=1, source_target_pairs={{64,0},{96,32},{128,64},{160,96},{192,128},{224,160},{256,192},{28... | collective-permute-start | bytes 884744 | tf_op jit(solution)/shard_map/ppermute | solution.py:17
  38.6 3.1 %collective-permute-done.3.second = bf16[960,128]{1,0:T(8,128)(2,1)S(1)} collective-permute-done((bf16[960,128]{1,0:T(8,128)(2,1)S(1)}, bf16[960,128]{1,0:T(8,128)(2,1)S(1)}, u32[]{:S(2)}, u32[]{:S(2)}) %collective-permute-start.3) | collective-permute-done | bytes 245792 | tf_op jit(solution)/shard_map/ppermute | solution.py:17
  41.7 1.5 %mid.1 = bf16[16,64,128]{2,1,0:T(8,128)(2,1)} custom-call(bf16[4,576,128]{2,1,0:T(8,128)(2,1)S(1)} %all-to-all-done.1.gathered, bf16[1,1,3,29,64,64]{5,4,3,2,1,0:T(8,128)(2,1)S(1)} %copy-done, bf16[960,128]{1,0:T(8,128)(2,1)S(1)} %collective-permute-done.2.first, bf16[960,128]{1,0:T(8,128)(2,1)S(1)} %collective-permute-done.3.second), custom_call_target="tpu_custom_call" | custom-call | flops 536870912 | bytes 3000000 | tf_op jit(solution)/shard_map/mid/pallas_call | solution.py:225
  43.1 7.6 %all-to-all-start.2 = ((bf16[16,64,128]{2,1,0:T(8,128)(2,1)}), bf16[16,64,128]{2,1,0:T(8,128)(2,1)S(1)}, u32[]{:S(2)}, u32[]{:S(2)}) async-start(bf16[16,64,128]{2,1,0:T(8,128)(2,1)} %mid.1), calls=%async_computation.2 | async-start | bytes 524288 | tf_op jit(solution)/shard_map/all_to_all | solution.py:233
  50.7 0.0 copy-start.2
  50.8 0.0 copy-start.3
  50.8 1.7 %copy-done.3 = bf16[1,1,9,384,384]{4,3,2,1,0:T(8,128)(2,1)S(1)} copy-done((bf16[1,1,9,384,384]{4,3,2,1,0:T(8,128)(2,1)S(1)}, bf16[1,1,9,384,384]{4,3,2,1,0:T(8,128)(2,1)}, u32[]{:S(2)}) %copy-start.3) | copy-done | bytes 2654232
  52.6 0.9 %copy-done.4 = bf16[1,16,64,64]{3,2,1,0:T(8,128)(2,1)S(1)} copy-done((bf16[1,16,64,64]{3,2,1,0:T(8,128)(2,1)S(1)}, bf16[1,16,64,64]{3,2,1,0:T(8,128)(2,1)}, u32[]{:S(2)}) %copy-start.4) | copy-done | bytes 131096
  53.5 2.2 %near.1 = (f32[128,384]{1,0:T(8,128)S(1)}, bf16[16,64,64]{2,1,0:T(8,128)(2,1)S(1)}) custom-call(s32[1,1,9]{2,1,0:T(1,128)S(1)} %copy-done.5, s32[1,1]{1,0:T(1,128)S(6)} %copy.12.count, s32[1,16]{1,0:T(1,128)S(1)} %copy-done.6, bf16[1,1,9,384,384]{4,3,2,1,0:T(8,128)(2,1)S(1)} %copy-done.3, bf16[3,128,384]{2,1,0:T(8,128)(2,1)S(1)} %pad_maximum_fusion.here, ...), custom_call_target="tpu_custom_call" | custom-call | flops 68719476736 | bytes 3538944 | tf_op jit(solution)/shard_map/near/pallas_call | solution.py:235
  55.7 6.7 %all-to-all-done.2.received = bf16[16,64,128]{2,1,0:T(8,128)(2,1)S(1)} async-done(((bf16[16,64,128]{2,1,0:T(8,128)(2,1)}), bf16[16,64,128]{2,1,0:T(8,128)(2,1)S(1)}, u32[]{:S(2)}, u32[]{:S(2)}) %all-to-all-start.2) | async-done | bytes 262176 | tf_op jit(solution)/shard_map/all_to_all | solution.py:233
  62.5 1.2 %final.1 = bf16[1,1,128,384]{3,2,1,0:T(8,128)(2,1)} custom-call(bf16[16,64,128]{2,1,0:T(8,128)(2,1)S(1)} %all-to-all-done.2.received, bf16[16,64,64]{2,1,0:T(8,128)(2,1)S(1)} %get-tuple-element.23.ordered, bf16[1,1,64,64]{3,2,1,0:T(8,128)(2,1)S(1)} %copy-done.2, bf16[1,1,64,384]{3,2,1,0:T(8,128)(2,1)S(1)} %copy-done.1, f32[128,384]{1,0:T(8,128)S(1)} %get-tuple-element.24.near), custom_call_target="tpu_custom_call" | custom-call | flops 29360128 | bytes 1000000 | tf_op jit(solution)/shard_map/final/pallas_call | solution.py:244
  (17 shorter events, 0.1 us)
Async XLA Ops:
  0.0 34.5 %copy-start.7 = (bf16[1,1,128,384]{3,2,1,0:T(8,128)(2,1)S(1)}, bf16[1,1,128,384]{3,2,1,0:T(8,128)(2,1)}, u32[]{:S(2)}) copy-start(bf16[1,1,128,384]{3,2,1,0:T(8,128)(2,1)} %vectors.1) | copy-start | bytes 294916
  0.0 28.0 %copy-start = (bf16[1,1,3,29,64,64]{5,4,3,2,1,0:T(8,128)(2,1)S(1)}, bf16[1,1,3,29,64,64]{5,4,3,2,1,0:T(8,128)(2,1)}, u32[]{:S(2)}) copy-start(bf16[1,1,3,29,64,64]{5,4,3,2,1,0:T(8,128)(2,1)} %own) | copy-start | bytes 2138116
  1.9 21.6 %all-to-all-start = ((bf16[8,96,128]{2,1,0:T(8,128)(2,1)}), bf16[8,96,128]{2,1,0:T(8,128)(2,1)S(1)}, u32[]{:S(2)}, u32[]{:S(2)}) async-start(bf16[8,96,128]{2,1,0:T(8,128)(2,1)} %leaf.1), calls=%async_computation | async-start | bytes 393216 | tf_op jit(solution)/shard_map/all_to_all | solution.py:194
  12.7 15.6 %collective-permute-start = (bf16[128,384]{1,0:T(8,128)(2,1)}, bf16[128,384]{1,0:T(8,128)(2,1)S(1)}, u32[]{:S(2)}, u32[]{:S(2)}) collective-permute-start(bf16[128,384]{1,0:T(8,128)(2,1)} %bitcast.4), channel_id=1, source_target_pairs={{1,0},{2,1},{3,2},{4,3},{5,4},{6,5},{7,6},{8,7},{9,8},{10,9},{11,1... | collective-permute-start | bytes 294920 | tf_op jit(solution)/shard_map/ppermute | solution.py:17
  19.5 8.8 %collective-permute-start.1 = (bf16[128,384]{1,0:T(8,128)(2,1)}, bf16[128,384]{1,0:T(8,128)(2,1)S(1)}, u32[]{:S(2)}, u32[]{:S(2)}) collective-permute-start(bf16[128,384]{1,0:T(8,128)(2,1)} %bitcast.5), channel_id=1, source_target_pairs={{2,0},{3,1},{4,2},{5,3},{6,4},{7,5},{8,6},{9,7},{10,8},{11,9},{12,... | collective-permute-start | bytes 294920 | tf_op jit(solution)/shard_map/ppermute | solution.py:17
  24.5 17.2 %all-to-all-start.1 = ((bf16[4,576,128]{2,1,0:T(8,128)(2,1)}), bf16[4,576,128]{2,1,0:T(8,128)(2,1)S(1)}, u32[]{:S(2)}, u32[]{:S(2)}) async-start(bf16[4,576,128]{2,1,0:T(8,128)(2,1)} %fold.1), calls=%async_computation.1 | async-start | bytes 1179648 | tf_op jit(solution)/shard_map/all_to_all | solution.py:205
  28.0 22.8 %copy-start.5 = (s32[1,1,9]{2,1,0:T(1,128)S(1)}, s32[1,1,9]{2,1,0:T(1,128)}, u32[]{:S(2)}) copy-start(s32[1,1,9]{2,1,0:T(1,128)} %source.1) | copy-start | bytes 112
  28.0 22.8 %copy-start.6 = (s32[1,16]{1,0:T(1,128)S(1)}, s32[1,16]{1,0:T(1,128)}, u32[]{:S(2)}) copy-start(s32[1,16]{1,0:T(1,128)} %listing.1) | copy-start | bytes 196
  28.3 10.2 %collective-permute-start.2 = (bf16[960,128]{1,0:T(8,128)(2,1)S(1)}, bf16[960,128]{1,0:T(8,128)(2,1)S(1)}, u32[]{:S(2)}, u32[]{:S(2)}) collective-permute-start(bf16[960,128]{1,0:T(8,128)(2,1)S(1)} %get-tuple-element.20), channel_id=1, source_target_pairs={{480,0},{0,32},{32,64},{64,96},{96,128},{128,160},{160,192},{192,2... | collective-permute-start | bytes 737288 | tf_op jit(solution)/shard_map/ppermute | solution.py:17
  31.3 10.3 %collective-permute-start.3 = (bf16[960,128]{1,0:T(8,128)(2,1)S(1)}, bf16[960,128]{1,0:T(8,128)(2,1)S(1)}, u32[]{:S(2)}, u32[]{:S(2)}) collective-permute-start(bf16[960,128]{1,0:T(8,128)(2,1)S(1)} %get-tuple-element.21), channel_id=1, source_target_pairs={{448,0},{480,32},{0,64},{32,96},{64,128},{96,160},{128,192},{160,2... | collective-permute-start | bytes 737288 | tf_op jit(solution)/shard_map/ppermute | solution.py:17
  34.6 16.2 %collective-permute-start.4 = (bf16[3,128,384]{2,1,0:T(8,128)(2,1)S(1)}, bf16[3,128,384]{2,1,0:T(8,128)(2,1)S(1)}, u32[]{:S(2)}, u32[]{:S(2)}) collective-permute-start(bf16[3,128,384]{2,1,0:T(8,128)(2,1)S(1)} %pad_maximum_fusion.here), channel_id=1, source_target_pairs={{32,0},{64,32},{96,64},{128,96},{160,128},{192,160},{224,192},{256... | collective-permute-start | bytes 884744 | tf_op jit(solution)/shard_map/ppermute | solution.py:17
  34.6 16.1 %collective-permute-start.5 = (bf16[3,128,384]{2,1,0:T(8,128)(2,1)S(1)}, bf16[3,128,384]{2,1,0:T(8,128)(2,1)S(1)}, u32[]{:S(2)}, u32[]{:S(2)}) collective-permute-start(bf16[3,128,384]{2,1,0:T(8,128)(2,1)S(1)} %pad_maximum_fusion.here), channel_id=1, source_target_pairs={{64,0},{96,32},{128,64},{160,96},{192,128},{224,160},{256,192},{28... | collective-permute-start | bytes 884744 | tf_op jit(solution)/shard_map/ppermute | solution.py:17
  43.1 19.3 %all-to-all-start.2 = ((bf16[16,64,128]{2,1,0:T(8,128)(2,1)}), bf16[16,64,128]{2,1,0:T(8,128)(2,1)S(1)}, u32[]{:S(2)}, u32[]{:S(2)}) async-start(bf16[16,64,128]{2,1,0:T(8,128)(2,1)} %mid.1), calls=%async_computation.2 | async-start | bytes 524288 | tf_op jit(solution)/shard_map/all_to_all | solution.py:233
  50.7 11.7 %copy-start.1 = (bf16[1,1,64,384]{3,2,1,0:T(8,128)(2,1)S(1)}, bf16[1,1,64,384]{3,2,1,0:T(8,128)(2,1)}, u32[]{:S(2)}) copy-start(bf16[1,1,64,384]{3,2,1,0:T(8,128)(2,1)} %basis.3) | copy-start | bytes 147460
  50.7 11.7 %copy-start.2 = (bf16[1,1,64,64]{3,2,1,0:T(8,128)(2,1)S(1)}, bf16[1,1,64,64]{3,2,1,0:T(8,128)(2,1)}, u32[]{:S(2)}) copy-start(bf16[1,1,64,64]{3,2,1,0:T(8,128)(2,1)} %transfer.3) | copy-start | bytes 24580
  50.8 1.8 %copy-start.3 = (bf16[1,1,9,384,384]{4,3,2,1,0:T(8,128)(2,1)S(1)}, bf16[1,1,9,384,384]{4,3,2,1,0:T(8,128)(2,1)}, u32[]{:S(2)}) copy-start(bf16[1,1,9,384,384]{4,3,2,1,0:T(8,128)(2,1)} %blocks.1) | copy-start | bytes 7962628
  52.6 0.9 %copy-start.4 = (bf16[1,16,64,64]{3,2,1,0:T(8,128)(2,1)S(1)}, bf16[1,16,64,64]{3,2,1,0:T(8,128)(2,1)}, u32[]{:S(2)}) copy-start(bf16[1,16,64,64]{3,2,1,0:T(8,128)(2,1)} %coupling.1) | copy-start | bytes 393220
